TPU v7x, 256 devices: a whole 4x4x8 slice. The times are simulated.
256 devices in a mesh: exp: 64 (over z, x, core), seq: 4 (over y).
Axes of the slice: x: 4, y: 4, z: 8, core: 2. Of those that a mesh axis runs over, the one named last changes fastest.
Arguments:
- layer_output_gradient: bfloat16 [2048, 7168], P(('exp', 'seq')), may hold values from -24 to 24
- residual_input: bfloat16 [2048, 7168], P(('exp', 'seq')), may hold values from -6 to 6
- norm_scale_vector: bfloat16 [7168], replicated, may hold values from 0.5 to 1.5
- chosen_expert_index: int32 [2048, 8], P(('exp', 'seq')), may hold values from 0 to 63, all different within a row; in each aligned block of 32 rows (0 to 31, 32 to 63, ...) at most 8 rows name the same one
- routing_gate_weight: bfloat16 [2048, 8], P(('exp', 'seq')), may hold values from 0.099609375 to 0.59765625
- expert_gate_weight: bfloat16 [64, 7168, 1024], P('exp', None, 'seq'), may hold values from -0.0625 to 0.0625
- expert_up_weight: bfloat16 [64, 7168, 1024], P('exp', None, 'seq'), may hold values from -0.0625 to 0.0625
- expert_down_weight: bfloat16 [64, 1024, 7168], P('exp', 'seq'), may hold values from -0.1875 to 0.1875
- stored_gate_state: bfloat16 [64, 512, 1024], P('exp', None, 'seq'), may hold values from -6 to 6
- stored_up_state: bfloat16 [64, 512, 1024], P('exp', None, 'seq'), may hold values from -6 to 6
- attention_output: bfloat16 [2048, 16384], P(('exp', 'seq')), may hold values from -24 to 24
- saved_adapter_latent: bfloat16 [2048, 32], P(('exp', 'seq')), may hold values from -0.109375 to 0.109375
- adapter_up_matrix: bfloat16 [32, 7168], replicated, may hold values from -0.00048828125 to 0.00048828125
Outputs:
- hidden_state_gradient: bfloat16 [2048, 7168], P(('exp', 'seq'))
- adapter_down_gradient: float32 [16384, 32], P(('exp', 'seq'))
- adapter_up_gradient_transposed: float32 [7168, 32], P(('exp', 'seq'))
Inputs may be any that keep to these rules, and one draw needn't show every extreme that they name: `chosen_expert_index`: each row names 8 different experts. In each aligned block of 32 rows (the tokens of one index of exp) no expert is named by more than 8 rows, and in some block some expert is named by exactly 8 rows.
All inputs are finite; a program needn't handle non-finite values.
Results may differ from a plain program's by a relative error of at most 0.015.
Values may be sent and summed in bfloat16 or wider, within the bound.
A program may use at most 128 MiB of HBM per device.

v0:
```python
import jax
import jax.numpy as jnp
from jax import lax
from jax.sharding import PartitionSpec as P

ADAPTER_SCALE = 2.0
NORM_EPS = 1e-06


def silu_parts(gate_val):
    sigmoid_val = jax.nn.sigmoid(gate_val)
    return (gate_val * sigmoid_val, sigmoid_val * (1.0 + gate_val * (1.0 - sigmoid_val)))


def contract_trailing(left, right):
    return lax.dot_general(
        left, right, (((1,), (1,)), ((), ())), preferred_element_type=jnp.float32
    )


def contract_leading(left, right):
    return lax.dot_general(
        left, right, (((0,), (0,)), ((), ())), preferred_element_type=jnp.float32
    )


def per_device(
    layer_output_gradient,
    residual_input,
    norm_scale_vector,
    chosen_expert_index,
    routing_gate_weight,
    expert_gate_weight,
    expert_up_weight,
    expert_down_weight,
    stored_gate_state,
    stored_up_state,
    attention_output,
    saved_adapter_latent,
    adapter_up_matrix,
):
    model_width = layer_output_gradient.shape[1]
    experts = lax.axis_size("exp") * expert_gate_weight.shape[0]
    capacity = stored_gate_state.shape[1] // experts
    group_grad, group_ids, group_weights = (
        lax.all_gather(layer_output_gradient, "seq", axis=0, tiled=True),
        lax.all_gather(chosen_expert_index, "seq", axis=0, tiled=True),
        lax.all_gather(routing_gate_weight, "seq", axis=0, tiled=True),
    )
    group_size = group_grad.shape[0]
    top_count = group_ids.shape[1]
    labels = jnp.arange(experts, dtype=jnp.int32)
    named_by = jnp.sum((group_ids[:, :, None] == labels[None, None, :]).astype(jnp.int32), axis=1)
    before = jnp.cumsum(named_by, axis=0) - named_by
    position = jnp.take_along_axis(before, group_ids, axis=1)
    slot_index = (group_ids * capacity + position).reshape(-1).astype(jnp.int32)
    token_ids = jnp.repeat(jnp.arange(group_size, dtype=jnp.int32), top_count)
    slot_owner = (
        jnp.full((experts * capacity,), group_size, jnp.int32).at[slot_index].set(token_ids)
    )
    padded = jnp.concatenate([group_grad, jnp.zeros((1, model_width), group_grad.dtype)], axis=0)
    outgoing = padded[slot_owner].reshape(experts, capacity, model_width)
    incoming = lax.all_to_all(outgoing, "exp", split_axis=0, concat_axis=0, tiled=True)
    slot_rows = incoming.reshape(-1, model_width)
    hidden_grad = contract_trailing(slot_rows, expert_down_weight[0])
    activation, silu_slope = silu_parts(stored_gate_state[0].astype(jnp.float32))
    gate_grad = (hidden_grad * stored_up_state[0].astype(jnp.float32) * silu_slope).astype(
        jnp.bfloat16
    )
    up_grad = (hidden_grad * activation).astype(jnp.bfloat16)
    partial_value = (
        contract_trailing(gate_grad, expert_gate_weight[0])
        + contract_trailing(up_grad, expert_up_weight[0])
    ).astype(jnp.bfloat16)
    sources = partial_value.shape[0] // capacity
    weights = group_weights.astype(jnp.float32)
    returned = lax.all_to_all(
        partial_value.reshape(sources, capacity, model_width),
        "exp",
        split_axis=0,
        concat_axis=0,
        tiled=True,
    )
    combine_returned = returned.reshape(experts * capacity, model_width)
    picked = combine_returned[slot_index].reshape(group_size, top_count, -1).astype(jnp.float32)
    combined = jnp.sum(picked * weights[:, :, None], axis=1)
    moe_grad = lax.psum_scatter(
        combined.astype(jnp.bfloat16), "seq", scatter_dimension=0, tiled=True
    ).astype(jnp.float32)
    residual = residual_input.astype(jnp.float32)
    inverse_rms = lax.rsqrt(jnp.mean(residual * residual, axis=1, keepdims=True) + NORM_EPS)
    scaled = norm_scale_vector.astype(jnp.float32)[None, :] * moe_grad
    inner_mean = jnp.mean(scaled * residual, axis=1, keepdims=True)
    hidden_state_gradient = (
        layer_output_gradient.astype(jnp.float32)
        + inverse_rms * scaled
        - residual * inner_mean * inverse_rms**3
    ).astype(jnp.bfloat16)
    adapter_latent_value = (
        ADAPTER_SCALE * contract_trailing(hidden_state_gradient, adapter_up_matrix)
    ).astype(jnp.bfloat16)
    down_contribution = contract_leading(attention_output, adapter_latent_value)
    up_contribution = ADAPTER_SCALE * contract_leading(hidden_state_gradient, saved_adapter_latent)
    complete_down_matrix, complete_up_matrix = lax.psum(
        (down_contribution, up_contribution), ("exp", "seq")
    )
    slot_member = lax.axis_index(("exp", "seq"))
    members = lax.axis_size(("exp", "seq"))
    down_projection_rows = complete_down_matrix.shape[0] // members
    up_projection_rows = complete_up_matrix.shape[0] // members
    adapter_down_gradient = lax.dynamic_slice_in_dim(
        complete_down_matrix, slot_member * down_projection_rows, down_projection_rows, 0
    )
    adapter_up_gradient_transposed = lax.dynamic_slice_in_dim(
        complete_up_matrix, slot_member * up_projection_rows, up_projection_rows, 0
    )
    return (hidden_state_gradient, adapter_down_gradient, adapter_up_gradient_transposed)


def solution(mesh):
    return jax.shard_map(
        per_device,
        mesh=mesh,
        in_specs=(
            P(("exp", "seq"), None),
            P(("exp", "seq"), None),
            P(),
            P(("exp", "seq"), None),
            P(("exp", "seq"), None),
            P("exp", None, "seq"),
            P("exp", None, "seq"),
            P("exp", "seq", None),
            P("exp", None, "seq"),
            P("exp", None, "seq"),
            P(("exp", "seq"), None),
            P(("exp", "seq"), None),
            P(),
        ),
        out_specs=(P(("exp", "seq"), None), P(("exp", "seq"), None), P(("exp", "seq"), None)),
        check_vma=False,
    )
```

profile of v0, /device:TPU:51, one launch (start us, length us, event | category | flops | bytes accessed | tf_op | source)
XLA Modules:
  0.0 731.7 jit_solution(16224991714569872756)
XLA Ops:
  7.2 0.0 copy-start
  7.2 8.1 %all_gather.10 = s32[32,8]{1,0:T(8,128)S(1)} all-gather(s32[8,8]{1,0:T(8,128)} %param.16), channel_id=1, replica_groups=mesh['exp'=64,'seq'=4] {'seq'}, dimensions={0}, use_global_device_ids=true | all-gather | bytes 1280 | tf_op jit(solution)/shard_map/all_gather | solution.py:47
  15.3 0.1 convert_reduce_fusion
  15.4 0.1 reduce_window_sum.11
  15.5 0.1 reshape.115
  15.6 0.0 copy-start.6
  15.6 1.9 gather_fusion.2
  17.5 0.1 reshape.118
  17.6 0.1 reshape.90
  17.7 0.1 reshape.125
  17.8 1.4 scatter_custom_fusion
  19.3 0.0 copy-done.6
  19.3 9.8 %all_gather.9 = bf16[32,7168]{1,0:T(8,128)(2,1)S(1)} all-gather(bf16[8,7168]{1,0:T(8,128)(2,1)S(1)} %copy-done.6), channel_id=1, replica_groups=mesh['exp'=64,'seq'=4] {'seq'}, dimensions={0}, use_global_device_ids=true | all-gather | bytes 573440 | tf_op jit(solution)/shard_map/all_gather | solution.py:46
  29.1 7.1 gather_fusion
  36.1 0.0 copy-start.12
  36.1 180.1 %all_to_all.10 = bf16[64,8,7168]{2,1,0:T(8,128)(2,1)S(1)} all-to-all(bf16[64,8,7168]{2,1,0:T(8,128)(2,1)} %bitcast.47), channel_id=1, replica_groups=mesh['exp'=64,'seq'=4] {'exp'}, dimensions={0} | all-to-all | bytes 14680064 | tf_op jit(solution)/shard_map/all_to_all | solution.py:63
  216.2 0.0 copy-done.12
  216.2 0.0 copy-start.1
  216.2 0.0 copy-start.3
  216.2 0.0 copy-start.7
  216.2 2.1 fusion.2
  218.3 0.0 copy-done.1
  218.4 0.0 copy-done.3
  218.4 0.0 copy-done.7
  218.4 0.0 copy-start.2
  218.4 7.4 %fusion.5 = f32[512,7168]{1,0:T(8,128)} fusion(bf16[1,7168,256]{2,1,0:T(8,128)(2,1)S(1)} %copy-done.1, f32[512,256]{1,0:T(8,128)S(1)} %fusion.2, bf16[1,512,256]{2,1,0:T(8,128)(2,1)S(1)} %copy-done.7, bf16[1,512,256]{2,1,0:T(8,128)(2,1)S(1)} %copy-done.3), kind=kOutput, calls=%fused_computation.13 | convolution fusion | flops 1880621056 | bytes 19398656 | tf_op jit(solution)/shard_map/dot_general | solution.py:16
  225.8 0.0 copy-done.2
  225.8 10.3 %fusion = bf16[64,8,7168]{2,1,0:T(8,128)(2,1)} fusion(f32[512,7168]{1,0:T(8,128)} %fusion.5, bf16[1,7168,256]{2,1,0:T(8,128)(2,1)S(1)} %copy-done.2, f32[512,256]{1,0:T(8,128)S(1)} %fusion.2, bf16[1,512,256]{2,1,0:T(8,128)(2,1)S(1)} %copy-done.3), kind=kOutput, calls=%fused_computation.6 | convolution fusion | flops 1887305728 | bytes 26476544 | tf_op jit(solution)/shard_map/dot_general | solution.py:16
  236.1 0.0 copy-start.11
  236.1 7.4 %all-to-all-start.1 = ((bf16[64,8,7168]{2,1,0:T(8,128)(2,1)}), bf16[64,8,7168]{2,1,0:T(8,128)(2,1)}, u32[]{:S(2)}, u32[]{:S(2)}) async-start(bf16[64,8,7168]{2,1,0:T(8,128)(2,1)} %fusion), calls=%async_computation.1 | async-start | bytes 14680064 | tf_op jit(solution)/shard_map/all_to_all | solution.py:77
  243.5 0.0 reduce-scatter.2.cloned.1.call-start
  243.5 0.0 copy-done.11
  243.6 9.6 %all_gather.11 = bf16[32,8]{1,0:T(8,128)(2,1)S(1)} all-gather(bf16[8,8]{1,0:T(8,128)(2,1)S(1)} %copy-done.11), channel_id=1, replica_groups=mesh['exp'=64,'seq'=4] {'seq'}, dimensions={0}, use_global_device_ids=true | all-gather | bytes 640 | tf_op jit(solution)/shard_map/all_gather | solution.py:48
  253.1 153.6 %all-to-all-done.1 = bf16[64,8,7168]{2,1,0:T(8,128)(2,1)} async-done(((bf16[64,8,7168]{2,1,0:T(8,128)(2,1)}), bf16[64,8,7168]{2,1,0:T(8,128)(2,1)}, u32[]{:S(2)}, u32[]{:S(2)}) %all-to-all-start.1) | async-done | bytes 7340064 | tf_op jit(solution)/shard_map/all_to_all | solution.py:77
  406.7 12.1 %gather_fusion.1 = bf16[256,7168]{1,0:T(8,128)(2,1)} fusion(bf16[512,7168]{1,0:T(8,128)(2,1)} %bitcast.11, s32[1024]{0:T(1024)S(1)} %pad_clamp_fusion), kind=kCustom, calls=%fused_computation.1 | custom fusion | bytes 7341056 | tf_op jit(solution)/shard_map/gather | solution.py:85
  418.9 0.0 copy-start.9
  418.9 0.0 copy-start.5
  418.9 0.0 copy-start.10
  418.9 0.0 copy-start.8
  418.9 5.5 fusion.1
  424.4 0.0 reduce-scatter.2.cloned.1.call-update
  424.4 0.0 all-reduce.4.cloned.1.call-start
  424.4 0.0 copy-done.9
  424.5 18.8 %reduce-scatter.2.cloned.1.call-done = bf16[8,7168]{1,0:T(8,128)(2,1)} async-done(((bf16[32,7168]{1,0:T(8,128)(2,1)}), bf16[8,7168]{1,0:T(8,128)(2,1)}) %reduce-scatter.2.cloned.1.call-update) | async-done | bytes 114704 | tf_op jit(solution)/shard_map/reduce_scatter | solution.py:87
  443.2 0.0 copy-done.5
  443.2 1.1 fusion.26
  444.3 1.0 fusion.29
  445.4 0.0 copy-done.10
  445.4 0.0 copy-start.4
  445.4 2.7 convolution_multiply_fusion
  448.1 0.0 copy-done
  448.1 0.0 copy-done.8
  448.1 2.3 convolution_bitcast_fusion
  450.3 0.0 all-reduce.4.cloned.1.call-update
  450.4 0.0 copy-done.4
  450.4 271.7 %all-reduce.4.cloned.1.call-done = (f32[16384,32]{0,1:T(8,128)}, f32[7168,32]{1,0:T(8,128)}) async-done(((f32[16384,32]{0,1:T(8,128)}, f32[7168,32]{1,0:T(8,128)}), (f32[16384,32]{0,1:T(8,128)}, f32[7168,32]{1,0:T(8,128)})) %all-reduce.4.cloned.1.call-update) | async-done | bytes 3014672 | tf_op jit(solution)/shard_map/psum | solution.py:104
  722.1 1.3 constant_dynamic-slice_fusion
  723.4 1.4 constant_dynamic-slice_fusion.1
  (12 shorter events, 0.1 us)
Async XLA Ops:
  7.2 440.9 %copy-start = (bf16[32,7168]{1,0:T(8,128)(2,1)S(1)}, bf16[32,7168]{1,0:T(8,128)(2,1)}, u32[]{:S(2)}) copy-start(bf16[32,7168]{1,0:T(8,128)(2,1)} %param.25) | copy-start | bytes 1376260
  15.6 3.7 copy-start.6
  36.1 180.1 %copy-start.12 = (bf16[1,256,7168]{2,1,0:T(8,128)(2,1)S(1)}, bf16[1,256,7168]{2,1,0:T(8,128)(2,1)}, u32[]{:S(2)}) copy-start(bf16[1,256,7168]{2,1,0:T(8,128)(2,1)} %param.20) | copy-start | bytes 11010052
  216.2 2.1 copy-start.1
  216.2 2.1 copy-start.3
  216.2 2.1 copy-start.7
  218.4 7.4 %copy-start.2 = (bf16[1,7168,256]{2,1,0:T(8,128)(2,1)S(1)}, bf16[1,7168,256]{2,1,0:T(8,128)(2,1)}, u32[]{:S(2)}) copy-start(bf16[1,7168,256]{2,1,0:T(8,128)(2,1)} %param.19) | copy-start | bytes 11010052
  236.1 7.5 %copy-start.11 = (bf16[8,8]{1,0:T(8,128)(2,1)S(1)}, bf16[8,8]{1,0:T(8,128)(2,1)}, u32[]{:S(2)}) copy-start(bf16[8,8]{1,0:T(8,128)(2,1)} %param.17) | copy-start | bytes 388
  236.1 170.7 %all-to-all-start.1 = ((bf16[64,8,7168]{2,1,0:T(8,128)(2,1)}), bf16[64,8,7168]{2,1,0:T(8,128)(2,1)}, u32[]{:S(2)}, u32[]{:S(2)}) async-start(bf16[64,8,7168]{2,1,0:T(8,128)(2,1)} %fusion), calls=%async_computation.1 | async-start | bytes 14680064 | tf_op jit(solution)/shard_map/all_to_all | solution.py:77
  243.5 199.7 %reduce-scatter.2.cloned.1.call-start = ((), (), s32[]{:S(2)}) async-start(), calls=%async_computation.3 | async-start | bytes 573440 | tf_op jit(solution)/shard_map/reduce_scatter | solution.py:87
  418.9 5.6 copy-start.9
  418.9 24.3 %copy-start.5 = (bf16[8,7168]{1,0:T(8,128)(2,1)S(1)}, bf16[8,7168]{1,0:T(8,128)(2,1)}, u32[]{:S(2)}) copy-start(bf16[8,7168]{1,0:T(8,128)(2,1)} %param.14) | copy-start | bytes 344068
  418.9 26.5 %copy-start.10 = (bf16[8,32]{1,0:T(8,128)(2,1)S(1)}, bf16[8,32]{1,0:T(8,128)(2,1)}, u32[]{:S(2)}) copy-start(bf16[8,32]{1,0:T(8,128)(2,1)} %param.24) | copy-start | bytes 1540
  418.9 29.2 %copy-start.8 = (bf16[8,16384]{1,0:T(8,128)(2,1)S(1)}, bf16[8,16384]{1,0:T(8,128)(2,1)}, u32[]{:S(2)}) copy-start(bf16[8,16384]{1,0:T(8,128)(2,1)} %param.23) | copy-start | bytes 786436
  424.4 297.7 %all-reduce.4.cloned.1.call-start = ((), (), s32[]{:S(2)}) async-start(), calls=%async_computation.4 | async-start | bytes 11534336 | tf_op jit(solution)/shard_map/psum | solution.py:104
  445.4 5.0 copy-start.4
Sparse Core Ops, SparseCore 0:
  424.5 18.6 reduce-scatter.1
  450.5 271.5 all-reduce.3
where the time goes:
time: 737 us; the launch traced here: 732 us
  waiting for transfers between devices  444 us (60%)
  blocking collectives  208 us (28%)
  local copies, waits for them, and re-layouts  25.7 us (3%)
  matrix products  24.7 us (3%)
  between operations  14.3 us (2%)
  other arithmetic  7.84 us (1%)
  starting transfers between devices  7.49 us (1%)
    psum x1, waiting for transfers between devices, per_device(): lax.psum((down_contribution, up_contribution), ('exp', 'seq'))  272 us
    all_to_all x1, blocking collectives, per_device(): lax.all_to_all(outgoing, 'exp', split_axis=0, concat_axis=0, tiled=True)  180 us
    all_to_all x1, waiting for transfers between devices, per_device(): lax.all_to_all(partial_value.reshape(sources, capacity, model_width), 'ex...  154 us
    dot_general x3, matrix products, contract_trailing(): lax.dot_general(left, right, (((1,), (1,)), ((), ())), preferred_element_...  19.8 us
    reduce_scatter x1, waiting for transfers between devices, per_device(): lax.psum_scatter(combined.astype(jnp.bfloat16), 'seq', scatter_dimension=...  18.8 us
  transfers between devices with their start and end apart: 3, of which 3 were waited for; matrix products, arithmetic and copies ran while one was open for 0% of the time, Pallas kernels for 0%

commit v1 on v0

v1 whole, which is shorter than its diff:
```python
import jax
import jax.numpy as jnp
from jax import lax
from jax.sharding import PartitionSpec as P

ADAPTER_SCALE = 2.0
NORM_EPS = 1e-06
LANES = 128
CHUNKS = 2


def silu_parts(gate_val):
    sigmoid_val = jax.nn.sigmoid(gate_val)
    return (gate_val * sigmoid_val, sigmoid_val * (1.0 + gate_val * (1.0 - sigmoid_val)))


def contract_trailing(left, right):
    return lax.dot_general(
        left, right, (((1,), (1,)), ((), ())), preferred_element_type=jnp.float32
    )


def contract_leading(left, right):
    return lax.dot_general(
        left, right, (((0,), (0,)), ((), ())), preferred_element_type=jnp.float32
    )


def matmul(left, right):
    return lax.dot_general(
        left, right, (((1,), (0,)), ((), ())), preferred_element_type=jnp.float32
    )


def by_column(array, parts):
    rows, columns = array.shape
    return array.reshape(rows, parts, columns // parts).transpose(1, 0, 2)


def per_device(
    layer_output_gradient,
    residual_input,
    norm_scale_vector,
    chosen_expert_index,
    routing_gate_weight,
    expert_gate_weight,
    expert_up_weight,
    expert_down_weight,
    stored_gate_state,
    stored_up_state,
    attention_output,
    saved_adapter_latent,
    adapter_up_matrix,
):
    n_exp, n_seq = lax.axis_size("exp"), lax.axis_size("seq")
    my_exp, my_seq = lax.axis_index("exp"), lax.axis_index("seq")
    tokens, width = layer_output_gradient.shape
    top_count = chosen_expert_index.shape[1]
    rank = saved_adapter_latent.shape[1]
    experts = n_exp * expert_gate_weight.shape[0]
    capacity = stored_gate_state.shape[1] // experts
    heads_width = attention_output.shape[1]
    quarter, att_quarter = width // n_seq, heads_width // n_seq
    group = tokens * n_seq

    small = jnp.concatenate(
        [
            saved_adapter_latent,
            chosen_expert_index.astype(jnp.bfloat16),
            routing_gate_weight,
            jnp.zeros((tokens, LANES - rank - 2 * top_count), jnp.bfloat16),
        ],
        axis=1,
    )
    packed = jnp.concatenate(
        [
            by_column(layer_output_gradient, n_seq),
            by_column(residual_input, n_seq),
            by_column(attention_output, n_seq),
            jnp.broadcast_to(small[None], (n_seq, tokens, LANES)),
        ],
        axis=2,
    )
    packed = lax.all_to_all(packed, "seq", split_axis=0, concat_axis=0, tiled=True)
    packed = packed.reshape(group, -1)
    grad = packed[:, :quarter]
    residual = packed[:, quarter : 2 * quarter]
    attention = packed[:, 2 * quarter : 2 * quarter + att_quarter]
    small = packed[:, 2 * quarter + att_quarter :]
    latent = small[:, :rank]
    ids = small[:, rank : rank + top_count].astype(jnp.int32)
    weights = small[:, rank + top_count : rank + 2 * top_count].astype(jnp.float32)

    labels = jnp.arange(experts, dtype=jnp.int32)
    hits = (ids[:, :, None] == labels[None, None, :]).astype(jnp.float32)
    named = jnp.sum(hits, axis=1)
    named_weight = jnp.sum(hits * weights[:, :, None], axis=1)
    before = jnp.sum(
        jnp.where(
            jnp.arange(group)[:, None, None] > jnp.arange(group)[None, :, None], named[None], 0.0
        ),
        axis=1,
    )
    slot_of = jnp.where(named > 0.0, before.astype(jnp.int32), -1)
    taken = slot_of[:, :, None] == jnp.arange(capacity, dtype=jnp.int32)[None, None, :]
    taken = taken.reshape(group, experts * capacity)
    pick = taken.astype(jnp.bfloat16)
    spread = jnp.repeat(named_weight, capacity, axis=1)
    merge = jnp.where(taken, spread, 0.0).astype(jnp.bfloat16)

    piece = quarter // CHUNKS
    down = expert_down_weight[0]
    hidden_grad = None
    for chunk in range(CHUNKS):
        part = grad[:, chunk * piece : (chunk + 1) * piece]
        outgoing = contract_leading(pick, part).astype(jnp.bfloat16)
        outgoing = outgoing.reshape(experts, capacity, piece)
        incoming = lax.all_to_all(outgoing, "exp", split_axis=0, concat_axis=0, tiled=True)
        rows = lax.all_gather(incoming.reshape(-1, piece), "seq", axis=0)
        for source in range(n_seq):
            first = source * quarter + chunk * piece
            term = contract_trailing(rows[source], down[:, first : first + piece])
            hidden_grad = term if hidden_grad is None else hidden_grad + term

    activation, silu_slope = silu_parts(stored_gate_state[0].astype(jnp.float32))
    gate_grad = (hidden_grad * stored_up_state[0].astype(jnp.float32) * silu_slope).astype(
        jnp.bfloat16
    )
    up_grad = (hidden_grad * activation).astype(jnp.bfloat16)

    moe_parts = []
    for chunk in range(CHUNKS):
        pieces = []
        for source in range(n_seq):
            first = source * quarter + chunk * piece
            value = contract_trailing(
                gate_grad, expert_gate_weight[0, first : first + piece]
            ) + contract_trailing(up_grad, expert_up_weight[0, first : first + piece])
            pieces.append(value.astype(jnp.bfloat16))
        summed = lax.psum_scatter(jnp.stack(pieces), "seq", scatter_dimension=0, tiled=False)
        returned = lax.all_to_all(
            summed.reshape(experts, capacity, piece),
            "exp",
            split_axis=0,
            concat_axis=0,
            tiled=True,
        )
        moe_parts.append(matmul(merge, returned.reshape(experts * capacity, piece)))
    moe_grad = jnp.concatenate(moe_parts, axis=1)

    residual = residual.astype(jnp.float32)
    grad = grad.astype(jnp.float32)
    scale = lax.dynamic_slice_in_dim(norm_scale_vector, my_seq * quarter, quarter, 0)
    adapter = lax.dynamic_slice_in_dim(adapter_up_matrix, my_seq * quarter, quarter, 1)
    square_sum = lax.psum(jnp.sum(residual * residual, axis=1, keepdims=True), "seq")
    inverse_rms = lax.rsqrt(square_sum / width + NORM_EPS)
    scaled = scale.astype(jnp.float32)[None, :] * moe_grad
    inner_mean = lax.psum(jnp.sum(scaled * residual, axis=1, keepdims=True), "seq") / width
    hidden_state = (
        grad + inverse_rms * scaled - residual * inner_mean * inverse_rms**3
    ).astype(jnp.bfloat16)
    act = ADAPTER_SCALE * lax.psum(contract_trailing(hidden_state, adapter), "seq")
    act = act.astype(jnp.bfloat16)
    down_rows = contract_leading(attention, act).reshape(n_exp, att_quarter // n_exp, rank)
    up_rows = ADAPTER_SCALE * contract_leading(hidden_state, latent).reshape(
        n_exp, quarter // n_exp, rank
    )
    total = lax.psum_scatter(
        jnp.concatenate([down_rows, up_rows], axis=1), "exp", scatter_dimension=0, tiled=False
    )
    members = n_exp * n_seq
    route = [
        (member, (member % n_seq) * n_exp + member // n_seq) for member in range(members)
    ]
    total = lax.ppermute(total, ("exp", "seq"), route)
    hidden_rows = lax.all_to_all(
        hidden_state.reshape(n_seq, tokens, quarter),
        "seq",
        split_axis=0,
        concat_axis=0,
        tiled=True,
    )
    hidden_rows = hidden_rows.transpose(1, 0, 2).reshape(tokens, width)
    return (
        hidden_rows,
        total[: att_quarter // n_exp],
        total[att_quarter // n_exp :],
    )


def solution(mesh):
    return jax.shard_map(
        per_device,
        mesh=mesh,
        in_specs=(
            P(("exp", "seq"), None),
            P(("exp", "seq"), None),
            P(),
            P(("exp", "seq"), None),
            P(("exp", "seq"), None),
            P("exp", None, "seq"),
            P("exp", None, "seq"),
            P("exp", "seq", None),
            P("exp", None, "seq"),
            P("exp", None, "seq"),
            P(("exp", "seq"), None),
            P(("exp", "seq"), None),
            P(),
        ),
        out_specs=(P(("exp", "seq"), None), P(("exp", "seq"), None), P(("exp", "seq"), None)),
        check_vma=False,
    )
```

time: 737 us -> 483 us (0.66)
  waiting for transfers between devices: 444 us -> 282 us
  blocking collectives: 208 us -> 86.8 us
  starting transfers between devices: 7.49 us -> 43.6 us
  local copies, waits for them, and re-layouts: 25.7 us -> 5.95 us
  matrix products: 24.7 us -> 33.1 us
    psum x1 -> x0, waiting for transfers between devices: 272 us -> none  [per_device(): lax.psum((down_contribution, up_contribution), ('exp', 'seq'))]
    unnamed x2 -> x6, waiting for transfers between devices: 0.03 us -> 130 us
    all_to_all x1 -> x4, waiting for transfers between devices: 154 us -> 29 us  [the longest x2 23.4 us: per_device(): lax.all_to_all(summed.reshape(experts, capacity, piece), 'exp', split_axi...]
    all_to_all x1 -> x2, blocking collectives: 180 us -> 69.3 us  [per_device(): lax.all_to_all(outgoing, 'exp', split_axis=0, concat_axis=0, tiled=True)]
    all_gather x0 -> x2, waiting for transfers between devices: none -> 53.5 us  [per_device(): rows = lax.all_gather(incoming.reshape(-1, piece), 'seq', axis=0)]
    reduce_scatter x1 -> x2, waiting for transfers between devices: 18.8 us -> 67.3 us  [per_device(): lax.psum_scatter(jnp.stack(pieces), 'seq', scatter_dimension=0, tiled=False)]
    all_gather x3 -> x0, blocking collectives: 27.4 us -> none  [the longest x1 9.77 us: per_device(): lax.all_gather(layer_output_gradient, 'seq', axis=0, tiled=True)]
    all_to_all x1 -> x4, starting transfers between devices: 7.4 us -> 31.4 us  [the longest x2 21.4 us: per_device(): lax.all_to_all(summed.reshape(experts, capacity, piece), 'exp', split_axi...]
  transfers between devices with their start and end apart: 3 -> 10, of which waited for: 3 -> 8; matrix products, arithmetic and copies ran while one was open for 0% -> 5% of each run, Pallas kernels for 0% -> 0%
where the time goes in v1:
time: 483 us; the launch traced here: 477 us
  waiting for transfers between devices  282 us (58%)
  blocking collectives  86.8 us (18%)
  starting transfers between devices  43.6 us (9%)
  matrix products  33.1 us (7%)
  between operations  14.1 us (3%)
  other arithmetic  11.1 us (2%)
  local copies, waits for them, and re-layouts  5.95 us (1%)
    unnamed x6, waiting for transfers between devices  130 us
    all_to_all x2, blocking collectives, per_device(): lax.all_to_all(outgoing, 'exp', split_axis=0, concat_axis=0, tiled=True)  69.3 us
    reduce_scatter x2, waiting for transfers between devices, per_device(): lax.psum_scatter(jnp.stack(pieces), 'seq', scatter_dimension=0, tiled=False)  67.3 us
    all_gather x2, waiting for transfers between devices, per_device(): rows = lax.all_gather(incoming.reshape(-1, piece), 'seq', axis=0)  53.5 us
    dot_general x25, matrix products, contract_trailing(): lax.dot_general(left, right, (((1,), (1,)), ((), ())), preferred_element_...  30.3 us
    all_to_all x2, waiting for transfers between devices, per_device(): lax.all_to_all(summed.reshape(experts, capacity, piece), 'exp', split_axi...  23.4 us
    all_to_all x2, starting transfers between devices, per_device(): lax.all_to_all(summed.reshape(experts, capacity, piece), 'exp', split_axi...  21.4 us
    ppermute x1, starting transfers between devices, per_device(): total = lax.ppermute(total, ('exp', 'seq'), route)  11.9 us
  transfers between devices with their start and end apart: 10, of which 8 were waited for; matrix products, arithmetic and copies ran while one was open for 5% of the time, Pallas kernels for 0%

profile of v1, /device:TPU:51, one launch (start us, length us, event | category | flops | bytes accessed | tf_op | source)
XLA Modules:
  0.0 477.1 jit_solution(6267419600146930378)
XLA Ops:
  7.2 0.7 convert_element_type.88
  8.0 0.8 maximum_maximum_fusion
  8.8 1.8 pad_maximum_fusion.3
  10.6 4.2 all-to-all-start
  15.0 5.5 %all-to-all-done = bf16[4,8,7808]{2,1,0:T(8,128)(2,1)S(1)} async-done(((bf16[4,8,7808]{2,1,0:T(8,128)(2,1)}), bf16[4,8,7808]{2,1,0:T(8,128)(2,1)S(1)}, u32[]{:S(2)}, u32[]{:S(2)}) %all-to-all-start) | async-done | bytes 499744 | tf_op jit(solution)/shard_map/all_to_all | solution.py:84
  21.1 0.5 fusion.8
  21.6 37.6 %all_to_all.30 = bf16[64,8,896]{2,1,0:T(8,128)(2,1)} all-to-all(bf16[64,8,896]{2,1,0:T(8,128)(2,1)S(1)} %fusion.8), channel_id=1, replica_groups=mesh['exp'=64,'seq'=4] {'exp'}, dimensions={0} | all-to-all | bytes 1835008 | tf_op jit(solution)/shard_map/all_to_all | solution.py:118
  59.2 0.5 fusion.9
  59.7 31.7 %all_to_all.31 = bf16[64,8,896]{2,1,0:T(8,128)(2,1)} all-to-all(bf16[64,8,896]{2,1,0:T(8,128)(2,1)S(1)} %fusion.9), channel_id=1, replica_groups=mesh['exp'=64,'seq'=4] {'exp'}, dimensions={0} | all-to-all | bytes 1835008 | tf_op jit(solution)/shard_map/all_to_all | solution.py:118
  91.4 11.6 %all-gather.3.cloned.1.call-done = bf16[4,512,896]{2,1,0:T(8,128)(2,1)} async-done(((bf16[1,512,896]{2,1,0:T(8,128)(2,1)}), bf16[4,512,896]{2,1,0:T(8,128)(2,1)}) %all-gather.3.cloned.1.call-update) | async-done | bytes 3670032 | tf_op jit(solution)/shard_map/all_gather | solution.py:119
  103.0 1.9 fusion.10
  104.9 1.8 convolution_add_fusion.6
  106.7 1.5 convolution_add_fusion.5
  108.2 1.5 convolution_add_fusion.4
  109.7 41.9 %all-gather.5.cloned.1.call-done = bf16[4,512,896]{2,1,0:T(8,128)(2,1)} async-done(((bf16[1,512,896]{2,1,0:T(8,128)(2,1)}), bf16[4,512,896]{2,1,0:T(8,128)(2,1)}) %all-gather.5.cloned.1.call-update) | async-done | bytes 3670032 | tf_op jit(solution)/shard_map/all_gather | solution.py:119
  151.6 1.9 convolution_add_fusion.3
  153.5 1.8 convolution_add_fusion.2
  155.3 1.6 convolution_add_fusion.1
  157.0 1.6 fusion.19
  158.6 0.5 fusion.50
  159.1 0.5 fusion.47
  159.5 0.5 fusion.44
  160.0 0.5 fusion.41
  160.5 0.6 copy-done.2
  161.1 0.5 fusion
  161.6 0.5 fusion.1
  162.1 0.5 fusion.2
  162.5 0.5 fusion.3
  163.0 2.1 pad_maximum_fusion
  165.3 1.5 fusion.38
  166.8 1.5 fusion.4
  168.3 1.5 fusion.35
  169.8 1.5 fusion.5
  171.3 1.5 fusion.32
  172.8 1.5 fusion.6
  174.3 1.5 fusion.29
  175.8 1.5 fusion.7
  177.3 2.2 pad_maximum_fusion.1
  179.4 30.7 %reduce-scatter.6.cloned.1.call-done = bf16[1,512,896]{2,1,0:T(8,128)(2,1)} async-done(((bf16[4,512,896]{2,1,0:T(8,128)(2,1)}), bf16[1,512,896]{2,1,0:T(8,128)(2,1)}) %reduce-scatter.6.cloned.1.call-update) | async-done | bytes 917520 | tf_op jit(solution)/shard_map/reduce_scatter | solution.py:140
  210.2 10.7 %all-to-all-start.3 = ((bf16[64,8,896]{2,1,0:T(8,128)(2,1)}), bf16[64,8,896]{2,1,0:T(8,128)(2,1)S(1)}, u32[]{:S(2)}, u32[]{:S(2)}) async-start(bf16[64,8,896]{2,1,0:T(8,128)(2,1)} %bitcast.181), calls=%async_computation.4 | async-start | bytes 1835008 | tf_op jit(solution)/shard_map/all_to_all | solution.py:141
  220.9 36.6 %reduce-scatter.8.cloned.1.call-done = bf16[1,512,896]{2,1,0:T(8,128)(2,1)} async-done(((bf16[4,512,896]{2,1,0:T(8,128)(2,1)}), bf16[1,512,896]{2,1,0:T(8,128)(2,1)}) %reduce-scatter.8.cloned.1.call-update) | async-done | bytes 917520 | tf_op jit(solution)/shard_map/reduce_scatter | solution.py:140
  257.5 10.7 %all-to-all-start.4 = ((bf16[64,8,896]{2,1,0:T(8,128)(2,1)}), bf16[64,8,896]{2,1,0:T(8,128)(2,1)S(1)}, u32[]{:S(2)}, u32[]{:S(2)}) async-start(bf16[64,8,896]{2,1,0:T(8,128)(2,1)} %bitcast.180), calls=%async_computation.6 | async-start | bytes 1835008 | tf_op jit(solution)/shard_map/all_to_all | solution.py:141
  268.3 0.8 dynamic-slice_convert_fusion
  269.1 0.3 convolution_bitcast_fusion.1
  269.4 23.4 %all-to-all-done.4 = bf16[64,8,896]{2,1,0:T(8,128)(2,1)S(1)} async-done(((bf16[64,8,896]{2,1,0:T(8,128)(2,1)}), bf16[64,8,896]{2,1,0:T(8,128)(2,1)S(1)}, u32[]{:S(2)}, u32[]{:S(2)}) %all-to-all-start.4) | async-done | bytes 917536 | tf_op jit(solution)/shard_map/all_to_all | solution.py:141
  292.9 0.3 convolution_bitcast_fusion
  293.3 6.0 %all-reduce.1 = (f32[32,1]{0,1:T(1,128)S(1)}, f32[32,1]{0,1:T(1,128)S(1)}) all-reduce(f32[32,1]{0,1:T(1,128)S(1)} %bitcast.188, f32[32,1]{0,1:T(1,128)S(1)} %bitcast.187), channel_id=1, replica_groups=mesh['exp'=64,'seq'=4] {'seq'}, use_global_device_ids=true, to_apply=%region_1.0 | all-reduce | flops 64 | bytes 512 | tf_op jit(solution)/shard_map/psum | solution.py:155
  299.3 0.8 fusion.74
  300.1 1.1 convolution_multiply_fusion
  301.2 1.0 fusion.85
  302.3 11.6 %psum.23 = f32[32,32]{1,0:T(8,128)S(1)} all-reduce(f32[32,32]{1,0:T(8,128)S(1)} %fusion.85), channel_id=1, replica_groups=mesh['exp'=64,'seq'=4] {'seq'}, use_global_device_ids=true, to_apply=%region_9.10 | all-reduce | flops 1024 | bytes 8192 | tf_op jit(solution)/shard_map/psum | solution.py:162
  313.8 0.3 fusion.68
  314.1 0.4 reshape.93
  314.5 0.6 copy.39
  315.1 1.3 mul.115
  316.4 0.6 copy.40
  317.0 1.3 pad_maximum_fusion.2
  318.4 5.7 %all-to-all-start.5 = ((bf16[4,8,1792]{2,1,0:T(8,128)(2,1)}), bf16[4,8,1792]{2,1,0:T(8,128)(2,1)S(1)}, u32[]{:S(2)}, u32[]{:S(2)}) async-start(bf16[4,8,1792]{2,1,0:T(8,128)(2,1)} %bitcast.57), calls=%async_computation.7 | async-start | bytes 229376 | tf_op jit(solution)/shard_map/all_to_all | solution.py:176
  324.1 130.2 %reduce-scatter.10.cloned.1.call-done = f32[1,92,32]{1,2,0:T(8,128)} async-done(((f32[64,92,32]{1,2,0:T(8,128)}), f32[1,92,32]{1,2,0:T(8,128)}) %reduce-scatter.10.cloned.1.call-update) | async-done | bytes 11792
  454.2 11.9 %collective-permute-start = (f32[92,32]{0,1:T(8,128)}, f32[92,32]{0,1:T(8,128)S(1)}, u32[]{:S(2)}, u32[]{:S(2)}) collective-permute-start(f32[92,32]{0,1:T(8,128)} %bitcast.189), channel_id=1, source_target_pairs={{0,0},{1,64},{2,128},{3,192},{4,1},{5,65},{6,129},{7,193},{8,2},{9... | collective-permute-start | bytes 35336 | tf_op jit(solution)/shard_map/ppermute | solution.py:175
  466.2 2.4 collective-permute-done
  468.7 0.7 copy.41
  469.4 0.6 copy.44
  470.0 0.6 copy.45
  (40 shorter events, 1.6 us)
Async XLA Ops:
  7.2 294.1 %copy-start = (bf16[32,7168]{1,0:T(8,128)(2,1)S(1)}, bf16[32,7168]{1,0:T(8,128)(2,1)}, u32[]{:S(2)}) copy-start(bf16[32,7168]{1,0:T(8,128)(2,1)} %param.25) | copy-start | bytes 1376260
  10.6 9.9 %all-to-all-start = ((bf16[4,8,7808]{2,1,0:T(8,128)(2,1)}), bf16[4,8,7808]{2,1,0:T(8,128)(2,1)S(1)}, u32[]{:S(2)}, u32[]{:S(2)}) async-start(bf16[4,8,7808]{2,1,0:T(8,128)(2,1)} %pad_maximum_fusion.3), calls=%async_computation | async-start | bytes 999424 | tf_op jit(solution)/shard_map/all_to_all | solution.py:84
  14.9 88.2 %all-gather.3.cloned.1.call-start = ((), (), s32[]{:S(2)}) async-start(), calls=%async_computation.9 | async-start | bytes 4587520 | tf_op jit(solution)/shard_map/all_gather | solution.py:119
  59.2 92.4 %all-gather.5.cloned.1.call-start = ((), (), s32[]{:S(2)}) async-start(), calls=%async_computation.10 | async-start | bytes 4587520 | tf_op jit(solution)/shard_map/all_gather | solution.py:119
  91.4 118.8 %reduce-scatter.6.cloned.1.call-start = ((), (), s32[]{:S(2)}) async-start(), calls=%async_computation.11 | async-start | bytes 4587520 | tf_op jit(solution)/shard_map/reduce_scatter | solution.py:140
  103.0 3.7 copy-start.4
  109.7 47.3 %copy-start.5 = (bf16[1,512,256]{2,1,0:T(8,128)(2,1)S(1)}, bf16[1,512,256]{2,1,0:T(8,128)(2,1)}, u32[]{:S(2)}) copy-start(bf16[1,512,256]{2,1,0:T(8,128)(2,1)} %param.21) | copy-start | bytes 786436
  109.7 47.3 %copy-start.6 = (bf16[1,512,256]{2,1,0:T(8,128)(2,1)S(1)}, bf16[1,512,256]{2,1,0:T(8,128)(2,1)}, u32[]{:S(2)}) copy-start(bf16[1,512,256]{2,1,0:T(8,128)(2,1)} %param.22) | copy-start | bytes 786436
  151.6 3.7 copy-start.3
  155.3 3.3 copy-start.1
  159.1 2.0 copy-start.2
  165.1 92.4 %reduce-scatter.8.cloned.1.call-start = ((), (), s32[]{:S(2)}) async-start(), calls=%async_computation.12 | async-start | bytes 4587520 | tf_op jit(solution)/shard_map/reduce_scatter | solution.py:140
  210.2 47.3 %all-to-all-start.3 = ((bf16[64,8,896]{2,1,0:T(8,128)(2,1)}), bf16[64,8,896]{2,1,0:T(8,128)(2,1)S(1)}, u32[]{:S(2)}, u32[]{:S(2)}) async-start(bf16[64,8,896]{2,1,0:T(8,128)(2,1)} %bitcast.181), calls=%async_computation.4 | async-start | bytes 1835008 | tf_op jit(solution)/shard_map/all_to_all | solution.py:141
  257.5 35.4 %all-to-all-start.4 = ((bf16[64,8,896]{2,1,0:T(8,128)(2,1)}), bf16[64,8,896]{2,1,0:T(8,128)(2,1)S(1)}, u32[]{:S(2)}, u32[]{:S(2)}) async-start(bf16[64,8,896]{2,1,0:T(8,128)(2,1)} %bitcast.180), calls=%async_computation.6 | async-start | bytes 1835008 | tf_op jit(solution)/shard_map/all_to_all | solution.py:141
  268.2 186.0 %reduce-scatter.10.cloned.1.call-start = ((), (), s32[]{:S(2)}) async-start(), calls=%async_computation.13 | async-start | bytes 1064960
  318.4 147.8 %all-to-all-start.5 = ((bf16[4,8,1792]{2,1,0:T(8,128)(2,1)}), bf16[4,8,1792]{2,1,0:T(8,128)(2,1)S(1)}, u32[]{:S(2)}, u32[]{:S(2)}) async-start(bf16[4,8,1792]{2,1,0:T(8,128)(2,1)} %bitcast.57), calls=%async_computation.7 | async-start | bytes 229376 | tf_op jit(solution)/shard_map/all_to_all | solution.py:176
  454.2 14.3 %collective-permute-start = (f32[92,32]{0,1:T(8,128)}, f32[92,32]{0,1:T(8,128)S(1)}, u32[]{:S(2)}, u32[]{:S(2)}) collective-permute-start(f32[92,32]{0,1:T(8,128)} %bitcast.189), channel_id=1, source_target_pairs={{0,0},{1,64},{2,128},{3,192},{4,1},{5,65},{6,129},{7,193},{8,2},{9... | collective-permute-start | bytes 35336 | tf_op jit(solution)/shard_map/ppermute | solution.py:175
Sparse Core Ops, SparseCore 0:
  59.3 43.6 all-gather.2
  104.8 46.7 all-gather.4
  165.2 44.8 reduce-scatter.5
  212.6 44.8 reduce-scatter.7
  318.5 135.7 reduce-scatter.9

commit v2 on v1

--- a/solution.py
+++ b/solution.py
@@ -6,7 +6,8 @@
 ADAPTER_SCALE = 2.0
 NORM_EPS = 1e-06
 LANES = 128
-CHUNKS = 2
+OUT_TILES = (3, 5, 6)
+BACK_TILES = (6, 5, 3)
 
 
 def silu_parts(gate_val):
@@ -53,7 +54,7 @@
     adapter_up_matrix,
 ):
     n_exp, n_seq = lax.axis_size("exp"), lax.axis_size("seq")
-    my_exp, my_seq = lax.axis_index("exp"), lax.axis_index("seq")
+    my_seq = lax.axis_index("seq")
     tokens, width = layer_output_gradient.shape
     top_count = chosen_expert_index.shape[1]
     rank = saved_adapter_latent.shape[1]
@@ -108,19 +109,36 @@
     spread = jnp.repeat(named_weight, capacity, axis=1)
     merge = jnp.where(taken, spread, 0.0).astype(jnp.bfloat16)
 
-    piece = quarter // CHUNKS
+    att_piece, hid_piece = att_quarter // n_exp, quarter // n_exp
+    lora_left = jnp.concatenate(
+        [
+            attention.reshape(group, n_exp, att_piece),
+            jnp.broadcast_to(latent[:, None], (group, n_exp, rank)),
+            jnp.zeros((group, n_exp, LANES - att_piece - rank), jnp.bfloat16),
+        ],
+        axis=2,
+    ).transpose(1, 0, 2)
+
     down = expert_down_weight[0]
     hidden_grad = None
-    for chunk in range(CHUNKS):
-        part = grad[:, chunk * piece : (chunk + 1) * piece]
-        outgoing = contract_leading(pick, part).astype(jnp.bfloat16)
+    start = 0
+    for index, tiles in enumerate(OUT_TILES):
+        piece = tiles * LANES
+        outgoing = contract_leading(pick, grad[:, start : start + piece]).astype(jnp.bfloat16)
         outgoing = outgoing.reshape(experts, capacity, piece)
         incoming = lax.all_to_all(outgoing, "exp", split_axis=0, concat_axis=0, tiled=True)
+        last = index == len(OUT_TILES) - 1
+        if last:
+            incoming, lora_left = lax.optimization_barrier((incoming, lora_left))
         rows = lax.all_gather(incoming.reshape(-1, piece), "seq", axis=0)
+        if last:
+            lora_left = lax.all_to_all(lora_left, "exp", split_axis=0, concat_axis=0, tiled=True)
+            rows, lora_left = lax.optimization_barrier((rows, lora_left))
         for source in range(n_seq):
-            first = source * quarter + chunk * piece
+            first = source * quarter + start
             term = contract_trailing(rows[source], down[:, first : first + piece])
             hidden_grad = term if hidden_grad is None else hidden_grad + term
+        start += piece
 
     activation, silu_slope = silu_parts(stored_gate_state[0].astype(jnp.float32))
     gate_grad = (hidden_grad * stored_up_state[0].astype(jnp.float32) * silu_slope).astype(
@@ -128,46 +146,87 @@
     )
     up_grad = (hidden_grad * activation).astype(jnp.bfloat16)
 
-    moe_parts = []
-    for chunk in range(CHUNKS):
+    returned = []
+
+    def send_back(summed):
+        returned.append(
+            lax.all_to_all(
+                summed.reshape(experts, capacity, -1),
+                "exp",
+                split_axis=0,
+                concat_axis=0,
+                tiled=True,
+            )
+        )
+
+    start, summed = 0, None
+    for tiles in BACK_TILES:
+        piece = tiles * LANES
         pieces = []
         for source in range(n_seq):
-            first = source * quarter + chunk * piece
+            first = source * quarter + start
             value = contract_trailing(
                 gate_grad, expert_gate_weight[0, first : first + piece]
             ) + contract_trailing(up_grad, expert_up_weight[0, first : first + piece])
             pieces.append(value.astype(jnp.bfloat16))
-        summed = lax.psum_scatter(jnp.stack(pieces), "seq", scatter_dimension=0, tiled=False)
-        returned = lax.all_to_all(
-            summed.reshape(experts, capacity, piece),
-            "exp",
-            split_axis=0,
-            concat_axis=0,
-            tiled=True,
-        )
-        moe_parts.append(matmul(merge, returned.reshape(experts * capacity, piece)))
+        partial_value = jnp.stack(pieces)
+        if summed is not None:
+            partial_value, summed, returned = lax.optimization_barrier(
+                (partial_value, summed, returned)
+            )
+        following = lax.psum_scatter(partial_value, "seq", scatter_dimension=0, tiled=False)
+        if summed is not None:
+            send_back(summed)
+        start, summed = start + piece, following
+    send_back(summed)
+    moe_parts = [
+        matmul(merge, block.reshape(experts * capacity, -1)) for block in returned
+    ]
     moe_grad = jnp.concatenate(moe_parts, axis=1)
 
-    residual = residual.astype(jnp.float32)
-    grad = grad.astype(jnp.float32)
     scale = lax.dynamic_slice_in_dim(norm_scale_vector, my_seq * quarter, quarter, 0)
     adapter = lax.dynamic_slice_in_dim(adapter_up_matrix, my_seq * quarter, quarter, 1)
-    square_sum = lax.psum(jnp.sum(residual * residual, axis=1, keepdims=True), "seq")
-    inverse_rms = lax.rsqrt(square_sum / width + NORM_EPS)
+    residual_f32 = residual.astype(jnp.float32)
     scaled = scale.astype(jnp.float32)[None, :] * moe_grad
-    inner_mean = lax.psum(jnp.sum(scaled * residual, axis=1, keepdims=True), "seq") / width
+    sums = jnp.concatenate(
+        [
+            contract_trailing(grad, adapter),
+            contract_trailing(residual, adapter),
+            contract_trailing(scaled.astype(jnp.bfloat16), adapter),
+            jnp.sum(residual_f32 * residual_f32, axis=1, keepdims=True),
+            jnp.sum(scaled * residual_f32, axis=1, keepdims=True),
+            jnp.zeros((group, LANES - 3 * rank - 2), jnp.float32),
+        ],
+        axis=1,
+    )
+    sums = lax.psum(sums, "seq")
+    inverse_rms = lax.rsqrt(sums[:, 3 * rank : 3 * rank + 1] / width + NORM_EPS)
+    back = sums[:, 3 * rank + 1 : 3 * rank + 2] / width * inverse_rms**3
     hidden_state = (
-        grad + inverse_rms * scaled - residual * inner_mean * inverse_rms**3
+        grad.astype(jnp.float32) + inverse_rms * scaled - residual_f32 * back
     ).astype(jnp.bfloat16)
-    act = ADAPTER_SCALE * lax.psum(contract_trailing(hidden_state, adapter), "seq")
+    act = ADAPTER_SCALE * (
+        sums[:, :rank]
+        + inverse_rms * sums[:, 2 * rank : 3 * rank]
+        - back * sums[:, rank : 2 * rank]
+    )
     act = act.astype(jnp.bfloat16)
-    down_rows = contract_leading(attention, act).reshape(n_exp, att_quarter // n_exp, rank)
-    up_rows = ADAPTER_SCALE * contract_leading(hidden_state, latent).reshape(
-        n_exp, quarter // n_exp, rank
-    )
-    total = lax.psum_scatter(
-        jnp.concatenate([down_rows, up_rows], axis=1), "exp", scatter_dimension=0, tiled=False
-    )
+    lora_right = jnp.concatenate(
+        [
+            hidden_state.reshape(group, n_exp, hid_piece),
+            jnp.zeros((group, n_exp, att_piece - hid_piece), jnp.bfloat16),
+            jnp.broadcast_to(act[:, None], (group, n_exp, rank)),
+            jnp.zeros((group, n_exp, LANES - att_piece - rank), jnp.bfloat16),
+        ],
+        axis=2,
+    ).transpose(1, 0, 2)
+    lora_right = lax.all_to_all(lora_right, "exp", split_axis=0, concat_axis=0, tiled=True)
+    products = contract_leading(
+        lora_left.reshape(-1, LANES), lora_right.reshape(-1, LANES)
+    )
+    down_rows = products[:att_piece, att_piece : att_piece + rank]
+    up_rows = ADAPTER_SCALE * products[att_piece : att_piece + rank, :hid_piece].T
+    total = jnp.concatenate([down_rows, up_rows], axis=0)
     members = n_exp * n_seq
     route = [
         (member, (member % n_seq) * n_exp + member // n_seq) for member in range(members)
@@ -183,8 +242,8 @@
     hidden_rows = hidden_rows.transpose(1, 0, 2).reshape(tokens, width)
     return (
         hidden_rows,
-        total[: att_quarter // n_exp],
-        total[att_quarter // n_exp :],
+        total[:att_piece],
+        total[att_piece:],
     )
 
 

time: 483 us -> 386 us (0.80)
  waiting for transfers between devices: 282 us -> 145 us
  matrix products: 33.1 us -> 53.8 us
  starting transfers between devices: 43.6 us -> 59.9 us
    unnamed x6, waiting for transfers between devices: 130 us -> 0.1 us
    all_to_all x2 -> x5, waiting for transfers between devices: 23.4 us -> 68.7 us  [the longest x3 43.9 us: send_back(): lax.all_to_all(summed.reshape(experts, capacity, -1), 'exp', split_axis=0...]
    reduce_scatter x2 -> x3, waiting for transfers between devices: 67.3 us -> 32.5 us  [per_device(): lax.psum_scatter(partial_value, 'seq', scatter_dimension=0, tiled=False)]
    all_to_all x0 -> x1, blocking collectives: none -> 26.9 us  [per_device(): lax.all_to_all(lora_right, 'exp', split_axis=0, concat_axis=0, tiled=True)]
    all_gather x2 -> x3, waiting for transfers between devices: 53.5 us -> 28.2 us  [per_device(): rows = lax.all_gather(incoming.reshape(-1, piece), 'seq', axis=0)]
    all_to_all x2 -> x5, starting transfers between devices: 21.4 us -> 45.6 us  [the longest x3 32.1 us: send_back(): lax.all_to_all(summed.reshape(experts, capacity, -1), 'exp', split_axis=0...]
    dot_general x25 -> x39, matrix products: 30.3 us -> 50.7 us  [contract_trailing(): lax.dot_general(left, right, (((1,), (1,)), ((), ())), preferred_element_...]
    all_to_all x2, blocking collectives: 69.3 us -> 53.2 us  [per_device(): lax.all_to_all(outgoing, 'exp', split_axis=0, concat_axis=0, tiled=True)]
  transfers between devices with their start and end apart: 10 -> 14, of which waited for: 8 -> 10; matrix products, arithmetic and copies ran while one was open for 5% -> 11% of each run, Pallas kernels for 0% -> 0%
where the time goes in v2:
time: 386 us; the launch traced here: 384 us
  waiting for transfers between devices  145 us (38%)
  blocking collectives  91.3 us (24%)
  starting transfers between devices  59.9 us (16%)
  matrix products  53.8 us (14%)
  between operations  14.6 us (4%)
  other arithmetic  12.6 us (3%)
  local copies, waits for them, and re-layouts  7.49 us (2%)
    all_to_all x2, blocking collectives, per_device(): lax.all_to_all(outgoing, 'exp', split_axis=0, concat_axis=0, tiled=True)  53.2 us
    dot_general x39, matrix products, contract_trailing(): lax.dot_general(left, right, (((1,), (1,)), ((), ())), preferred_element_...  50.7 us
    all_to_all x3, waiting for transfers between devices, send_back(): lax.all_to_all(summed.reshape(experts, capacity, -1), 'exp', split_axis=0...  43.9 us
    reduce_scatter x3, waiting for transfers between devices, per_device(): lax.psum_scatter(partial_value, 'seq', scatter_dimension=0, tiled=False)  32.5 us
    all_to_all x3, starting transfers between devices, send_back(): lax.all_to_all(summed.reshape(experts, capacity, -1), 'exp', split_axis=0...  32.1 us
    all_gather x3, waiting for transfers between devices, per_device(): rows = lax.all_gather(incoming.reshape(-1, piece), 'seq', axis=0)  28.2 us
    all_to_all x1, blocking collectives, per_device(): lax.all_to_all(lora_right, 'exp', split_axis=0, concat_axis=0, tiled=True)  26.9 us
    all_to_all x1, waiting for transfers between devices, per_device(): lax.all_to_all(outgoing, 'exp', split_axis=0, concat_axis=0, tiled=True)  19.7 us
  transfers between devices with their start and end apart: 14, of which 10 were waited for; matrix products, arithmetic and copies ran while one was open for 11% of the time, Pallas kernels for 0%

profile of v2, /device:TPU:51, one launch (start us, length us, event | category | flops | bytes accessed | tf_op | source)
XLA Modules:
  0.0 384.5 jit_solution(8564104012834371837)
XLA Ops:
  8.8 1.8 pad_maximum_fusion.3
  10.6 4.2 %all-to-all-start = ((bf16[4,8,7808]{2,1,0:T(8,128)(2,1)}), bf16[4,8,7808]{2,1,0:T(8,128)(2,1)S(1)}, u32[]{:S(2)}, u32[]{:S(2)}) async-start(bf16[4,8,7808]{2,1,0:T(8,128)(2,1)} %pad_maximum_fusion.3), calls=%async_computation | async-start | bytes 999424 | tf_op jit(solution)/shard_map/all_to_all | solution.py:85
  15.0 5.5 %all-to-all-done = bf16[4,8,7808]{2,1,0:T(8,128)(2,1)S(1)} async-done(((bf16[4,8,7808]{2,1,0:T(8,128)(2,1)}), bf16[4,8,7808]{2,1,0:T(8,128)(2,1)S(1)}, u32[]{:S(2)}, u32[]{:S(2)}) %all-to-all-start) | async-done | bytes 499744 | tf_op jit(solution)/shard_map/all_to_all | solution.py:85
  21.4 27.2 %all_to_all.50 = bf16[64,8,384]{2,1,0:T(8,128)(2,1)} all-to-all(bf16[64,8,384]{2,1,0:T(8,128)(2,1)S(1)} %fusion.18), channel_id=1, replica_groups=mesh['exp'=64,'seq'=4] {'exp'}, dimensions={0} | all-to-all | bytes 786432 | tf_op jit(solution)/shard_map/all_to_all | solution.py:129
  49.1 26.0 %all_to_all.51 = bf16[64,8,640]{2,1,0:T(8,128)(2,1)} all-to-all(bf16[64,8,640]{2,1,0:T(8,128)(2,1)S(1)} %fusion.9), channel_id=1, replica_groups=mesh['exp'=64,'seq'=4] {'exp'}, dimensions={0} | all-to-all | bytes 1310720 | tf_op jit(solution)/shard_map/all_to_all | solution.py:129
  75.2 1.3 fusion.4
  76.5 6.5 %all-to-all-start.3 = ((bf16[64,8,768]{2,1,0:T(8,128)(2,1)}), bf16[64,8,768]{2,1,0:T(8,128)(2,1)S(1)}, u32[]{:S(2)}, u32[]{:S(2)}) async-start(bf16[64,8,768]{2,1,0:T(8,128)(2,1)} %fusion.4), calls=%async_computation.3 | async-start | bytes 1572864 | tf_op jit(solution)/shard_map/all_to_all | solution.py:129
  85.2 19.7 %all-to-all-done.3 = bf16[64,8,768]{2,1,0:T(8,128)(2,1)S(1)} async-done(((bf16[64,8,768]{2,1,0:T(8,128)(2,1)}), bf16[64,8,768]{2,1,0:T(8,128)(2,1)S(1)}, u32[]{:S(2)}, u32[]{:S(2)}) %all-to-all-start.3) | async-done | bytes 786464 | tf_op jit(solution)/shard_map/all_to_all | solution.py:129
  105.9 7.0 %all-to-all-start.4 = ((bf16[64,32,128]{2,1,0:T(8,128)(2,1)}), bf16[64,32,128]{2,1,0:T(8,128)(2,1)S(1)}, u32[]{:S(2)}, u32[]{:S(2)}) async-start(bf16[64,32,128]{2,1,0:T(8,128)(2,1)} %maximum_bitcast_fusion), calls=%async_computation.4 | async-start | bytes 1048576 | tf_op jit(solution)/shard_map/all_to_all | solution.py:135
  113.1 1.4 fusion.44
  114.5 1.4 convolution_add_fusion.18
  115.9 1.4 convolution_add_fusion.17
  117.3 1.4 convolution_add_fusion.16
  118.7 1.7 convolution_add_fusion.15
  120.4 1.6 convolution_add_fusion.14
  122.0 1.4 convolution_add_fusion.13
  123.4 1.4 convolution_add_fusion.12
  124.8 5.1 %all-to-all-done.4 = bf16[64,32,128]{2,1,0:T(8,128)(2,1)S(1)} async-done(((bf16[64,32,128]{2,1,0:T(8,128)(2,1)}), bf16[64,32,128]{2,1,0:T(8,128)(2,1)S(1)}, u32[]{:S(2)}, u32[]{:S(2)}) %all-to-all-start.4) | async-done | bytes 524320 | tf_op jit(solution)/shard_map/all_to_all | solution.py:135
  129.9 28.2 %all-gather.8.cloned.1.call-done = bf16[4,512,768]{2,1,0:T(8,128)(2,1)} async-done(((bf16[1,512,768]{2,1,0:T(8,128)(2,1)}), bf16[4,512,768]{2,1,0:T(8,128)(2,1)}) %all-gather.8.cloned.1.call-update) | async-done | bytes 3145744 | tf_op jit(solution)/shard_map/all_gather | solution.py:133
  158.1 1.8 convolution_add_fusion.11
  159.9 1.6 convolution_add_fusion.10
  161.6 1.4 convolution_add_fusion.9
  163.0 1.5 fusion.39
  164.5 1.4 fusion.55
  165.9 1.4 fusion.52
  167.3 1.4 fusion.49
  168.7 1.4 fusion.46
  170.1 1.4 fusion.5
  171.5 1.4 fusion.6
  172.9 1.4 fusion.7
  174.3 1.4 fusion.8
  175.8 1.9 pad_maximum_fusion
  177.7 1.4 fusion.79
  179.1 1.4 fusion.13
  180.5 1.4 fusion.76
  181.9 1.4 fusion.12
  183.2 1.4 fusion.73
  184.6 1.4 fusion.11
  186.0 1.4 fusion.70
  187.4 1.4 fusion.10
  188.8 1.9 pad_maximum_fusion.1
  190.7 27.7 %reduce-scatter.4.cloned.1.call-done = bf16[1,512,768]{2,1,0:T(8,128)(2,1)} async-done(((bf16[4,512,768]{2,1,0:T(8,128)(2,1)}), bf16[1,512,768]{2,1,0:T(8,128)(2,1)}) %reduce-scatter.4.cloned.1.call-update) | async-done | bytes 786448 | tf_op jit(solution)/shard_map/reduce_scatter | solution.py:177
  218.4 1.2 fusion.107
  219.7 10.7 %all-to-all-start.5 = ((bf16[64,8,768]{2,1,0:T(8,128)(2,1)}), bf16[64,8,768]{2,1,0:T(8,128)(2,1)S(1)}, u32[]{:S(2)}, u32[]{:S(2)}) async-start(bf16[64,8,768]{2,1,0:T(8,128)(2,1)} %bitcast.246), calls=%async_computation.7 | async-start | bytes 1572864 | tf_op jit(solution)/shard_map/all_to_all | solution.py:153
  230.5 1.3 fusion.22
  231.7 1.3 fusion.104
  233.0 1.3 fusion.21
  234.3 1.3 fusion.101
  235.6 1.3 fusion.20
  236.8 1.3 fusion.98
  238.1 1.3 fusion.19
  239.4 1.4 pad_maximum_fusion.2
  240.8 11.7 %all-to-all-done.5 = bf16[64,8,768]{2,1,0:T(8,128)(2,1)S(1)} async-done(((bf16[64,8,768]{2,1,0:T(8,128)(2,1)}), bf16[64,8,768]{2,1,0:T(8,128)(2,1)S(1)}, u32[]{:S(2)}, u32[]{:S(2)}) %all-to-all-start.5) | async-done | bytes 786464 | tf_op jit(solution)/shard_map/all_to_all | solution.py:153
  252.4 4.7 %reduce-scatter.6.cloned.1.call-done = bf16[1,512,640]{2,1,0:T(8,128)(2,1)} async-done(((bf16[4,512,640]{2,1,0:T(8,128)(2,1)}), bf16[1,512,640]{2,1,0:T(8,128)(2,1)}) %reduce-scatter.6.cloned.1.call-update) | async-done | bytes 655376 | tf_op jit(solution)/shard_map/reduce_scatter | solution.py:177
  257.2 10.9 %all-to-all-start.6 = ((bf16[64,8,640]{2,1,0:T(8,128)(2,1)}), bf16[64,8,640]{2,1,0:T(8,128)(2,1)S(1)}, u32[]{:S(2)}, u32[]{:S(2)}) async-start(bf16[64,8,640]{2,1,0:T(8,128)(2,1)} %bitcast.247), calls=%async_computation.8 | async-start | bytes 1310720 | tf_op jit(solution)/shard_map/all_to_all | solution.py:153
  268.1 19.7 %all-to-all-done.6 = bf16[64,8,640]{2,1,0:T(8,128)(2,1)S(1)} async-done(((bf16[64,8,640]{2,1,0:T(8,128)(2,1)}), bf16[64,8,640]{2,1,0:T(8,128)(2,1)S(1)}, u32[]{:S(2)}, u32[]{:S(2)}) %all-to-all-start.6) | async-done | bytes 655392 | tf_op jit(solution)/shard_map/all_to_all | solution.py:153
  287.9 10.4 %all-to-all-start.7 = ((bf16[64,8,384]{2,1,0:T(8,128)(2,1)}), bf16[64,8,384]{2,1,0:T(8,128)(2,1)S(1)}, u32[]{:S(2)}, u32[]{:S(2)}) async-start(bf16[64,8,384]{2,1,0:T(8,128)(2,1)} %bitcast.249), calls=%async_computation.10 | async-start | bytes 786432 | tf_op jit(solution)/shard_map/all_to_all | solution.py:153
  300.1 12.5 %all-to-all-done.7 = bf16[64,8,384]{2,1,0:T(8,128)(2,1)S(1)} async-done(((bf16[64,8,384]{2,1,0:T(8,128)(2,1)}), bf16[64,8,384]{2,1,0:T(8,128)(2,1)S(1)}, u32[]{:S(2)}, u32[]{:S(2)}) %all-to-all-start.7) | async-done | bytes 393248 | tf_op jit(solution)/shard_map/all_to_all | solution.py:153
  313.4 11.1 %psum.7 = f32[32,128]{1,0:T(8,128)S(1)} all-reduce(f32[32,128]{1,0:T(8,128)S(1)} %concatenate.25), channel_id=1, replica_groups=mesh['exp'=64,'seq'=4] {'seq'}, use_global_device_ids=true, to_apply=%region_8.9 | all-reduce | flops 4096 | bytes 32768 | tf_op jit(solution)/shard_map/psum | solution.py:202
  325.6 2.2 reshape.117
  328.7 26.9 %all_to_all.52 = bf16[64,32,128]{2,1,0:T(8,128)(2,1)S(1)} all-to-all(bf16[64,32,128]{2,1,0:T(8,128)(2,1)S(1)} %maximum_bitcast_fusion.1), channel_id=1, replica_groups=mesh['exp'=64,'seq'=4] {'exp'}, dimensions={0} | all-to-all | bytes 1048576 | tf_op jit(solution)/shard_map/all_to_all | solution.py:223
  355.6 5.7 %all-to-all-start.8 = ((bf16[4,8,1792]{2,1,0:T(8,128)(2,1)}), bf16[4,8,1792]{2,1,0:T(8,128)(2,1)S(1)}, u32[]{:S(2)}, u32[]{:S(2)}) async-start(bf16[4,8,1792]{2,1,0:T(8,128)(2,1)} %bitcast.77), calls=%async_computation.11 | async-start | bytes 229376 | tf_op jit(solution)/shard_map/all_to_all | solution.py:235
  361.8 4.1 %collective-permute-start = (f32[92,32]{0,1:T(8,128)S(1)}, f32[92,32]{0,1:T(8,128)S(1)}, u32[]{:S(2)}, u32[]{:S(2)}) collective-permute-start(f32[92,32]{0,1:T(8,128)S(1)} %pad_maximum_fusion.4), channel_id=1, source_target_pairs={{0,0},{1,64},{2,128},{3,192},{4,1},{5,65},{6,129},{7,193},{8,2},{9... | collective-permute-start | bytes 35336 | tf_op jit(solution)/shard_map/ppermute | solution.py:234
  365.9 9.7 %collective-permute-done = f32[92,32]{0,1:T(8,128)S(1)} collective-permute-done((f32[92,32]{0,1:T(8,128)S(1)}, f32[92,32]{0,1:T(8,128)S(1)}, u32[]{:S(2)}, u32[]{:S(2)}) %collective-permute-start) | collective-permute-done | bytes 11808 | tf_op jit(solution)/shard_map/ppermute | solution.py:234
  (85 shorter events, 13.7 us)
Async XLA Ops:
  7.2 292.1 %copy-start = (bf16[32,7168]{1,0:T(8,128)(2,1)S(1)}, bf16[32,7168]{1,0:T(8,128)(2,1)}, u32[]{:S(2)}) copy-start(bf16[32,7168]{1,0:T(8,128)(2,1)} %param.25) | copy-start | bytes 1376260
  10.6 9.9 %all-to-all-start = ((bf16[4,8,7808]{2,1,0:T(8,128)(2,1)}), bf16[4,8,7808]{2,1,0:T(8,128)(2,1)S(1)}, u32[]{:S(2)}, u32[]{:S(2)}) async-start(bf16[4,8,7808]{2,1,0:T(8,128)(2,1)} %pad_maximum_fusion.3), calls=%async_computation | async-start | bytes 999424 | tf_op jit(solution)/shard_map/all_to_all | solution.py:85
  14.9 98.3 %all-gather.4.cloned.1.call-start = ((), (), s32[]{:S(2)}) async-start(), calls=%async_computation.13 | async-start | bytes 1966080 | tf_op jit(solution)/shard_map/all_gather | solution.py:133
  48.7 70.0 %all-gather.6.cloned.1.call-start = ((), (), s32[]{:S(2)}) async-start(), calls=%async_computation.14 | async-start | bytes 3276800 | tf_op jit(solution)/shard_map/all_gather | solution.py:133
  76.5 28.5 %all-to-all-start.3 = ((bf16[64,8,768]{2,1,0:T(8,128)(2,1)}), bf16[64,8,768]{2,1,0:T(8,128)(2,1)S(1)}, u32[]{:S(2)}, u32[]{:S(2)}) async-start(bf16[64,8,768]{2,1,0:T(8,128)(2,1)} %fusion.4), calls=%async_computation.3 | async-start | bytes 1572864 | tf_op jit(solution)/shard_map/all_to_all | solution.py:129
  82.9 75.1 %all-gather.8.cloned.1.call-start = ((), (), s32[]{:S(2)}) async-start(), calls=%async_computation.15 | async-start | bytes 3932160 | tf_op jit(solution)/shard_map/all_gather | solution.py:133
  104.9 0.9 copy-start.1
  105.9 24.0 %all-to-all-start.4 = ((bf16[64,32,128]{2,1,0:T(8,128)(2,1)}), bf16[64,32,128]{2,1,0:T(8,128)(2,1)S(1)}, u32[]{:S(2)}, u32[]{:S(2)}) async-start(bf16[64,32,128]{2,1,0:T(8,128)(2,1)} %maximum_bitcast_fusion), calls=%async_computation.4 | async-start | bytes 1048576 | tf_op jit(solution)/shard_map/all_to_all | solution.py:135
  112.9 105.5 %reduce-scatter.4.cloned.1.call-start = ((), (), s32[]{:S(2)}) async-start(), calls=%async_computation.16 | async-start | bytes 3932160 | tf_op jit(solution)/shard_map/reduce_scatter | solution.py:177
  118.7 3.3 copy-start.2
  124.8 38.2 %copy-start.6 = (bf16[1,512,256]{2,1,0:T(8,128)(2,1)S(1)}, bf16[1,512,256]{2,1,0:T(8,128)(2,1)}, u32[]{:S(2)}) copy-start(bf16[1,512,256]{2,1,0:T(8,128)(2,1)} %param.21) | copy-start | bytes 786436
  124.8 38.2 %copy-start.7 = (bf16[1,512,256]{2,1,0:T(8,128)(2,1)S(1)}, bf16[1,512,256]{2,1,0:T(8,128)(2,1)}, u32[]{:S(2)}) copy-start(bf16[1,512,256]{2,1,0:T(8,128)(2,1)} %param.22) | copy-start | bytes 786436
  129.9 30.0 %copy-start.4 = (bf16[64,32,128]{2,1,0:T(8,128)(2,1)}, bf16[64,32,128]{2,1,0:T(8,128)(2,1)S(1)}, u32[]{:S(2)}) copy-start(bf16[64,32,128]{2,1,0:T(8,128)(2,1)S(1)} %all-to-all-done.4) | copy-start | bytes 1572868
  158.1 3.4 copy-start.3
  177.6 79.5 %reduce-scatter.6.cloned.1.call-start = ((), (), s32[]{:S(2)}) async-start(), calls=%async_computation.17 | async-start | bytes 3276800 | tf_op jit(solution)/shard_map/reduce_scatter | solution.py:177
  219.7 32.7 %all-to-all-start.5 = ((bf16[64,8,768]{2,1,0:T(8,128)(2,1)}), bf16[64,8,768]{2,1,0:T(8,128)(2,1)S(1)}, u32[]{:S(2)}, u32[]{:S(2)}) async-start(bf16[64,8,768]{2,1,0:T(8,128)(2,1)} %bitcast.246), calls=%async_computation.7 | async-start | bytes 1572864 | tf_op jit(solution)/shard_map/all_to_all | solution.py:153
  230.4 57.4 %reduce-scatter.8.cloned.1.call-start = ((), (), s32[]{:S(2)}) async-start(), calls=%async_computation.18 | async-start | bytes 1966080 | tf_op jit(solution)/shard_map/reduce_scatter | solution.py:177
  257.2 30.7 %all-to-all-start.6 = ((bf16[64,8,640]{2,1,0:T(8,128)(2,1)}), bf16[64,8,640]{2,1,0:T(8,128)(2,1)S(1)}, u32[]{:S(2)}, u32[]{:S(2)}) async-start(bf16[64,8,640]{2,1,0:T(8,128)(2,1)} %bitcast.247), calls=%async_computation.8 | async-start | bytes 1310720 | tf_op jit(solution)/shard_map/all_to_all | solution.py:153
  287.9 24.7 %all-to-all-start.7 = ((bf16[64,8,384]{2,1,0:T(8,128)(2,1)}), bf16[64,8,384]{2,1,0:T(8,128)(2,1)S(1)}, u32[]{:S(2)}, u32[]{:S(2)}) async-start(bf16[64,8,384]{2,1,0:T(8,128)(2,1)} %bitcast.249), calls=%async_computation.10 | async-start | bytes 786432 | tf_op jit(solution)/shard_map/all_to_all | solution.py:153
  313.0 48.3 %copy-start.5 = (bf16[64,32,128]{2,1,0:T(8,128)(2,1)S(1)}, bf16[64,32,128]{2,1,0:T(8,128)(2,1)}, u32[]{:S(2)}) copy-start(bf16[64,32,128]{2,1,0:T(8,128)(2,1)} %copy-done.4) | copy-start | bytes 1572868
  355.6 10.3 %all-to-all-start.8 = ((bf16[4,8,1792]{2,1,0:T(8,128)(2,1)}), bf16[4,8,1792]{2,1,0:T(8,128)(2,1)S(1)}, u32[]{:S(2)}, u32[]{:S(2)}) async-start(bf16[4,8,1792]{2,1,0:T(8,128)(2,1)} %bitcast.77), calls=%async_computation.11 | async-start | bytes 229376 | tf_op jit(solution)/shard_map/all_to_all | solution.py:235
  361.8 13.8 %collective-permute-start = (f32[92,32]{0,1:T(8,128)S(1)}, f32[92,32]{0,1:T(8,128)S(1)}, u32[]{:S(2)}, u32[]{:S(2)}) collective-permute-start(f32[92,32]{0,1:T(8,128)S(1)} %pad_maximum_fusion.4), channel_id=1, source_target_pairs={{0,0},{1,64},{2,128},{3,192},{4,1},{5,65},{6,129},{7,193},{8,2},{9... | collective-permute-start | bytes 35336 | tf_op jit(solution)/shard_map/ppermute | solution.py:234
Sparse Core Ops, SparseCore 0:
  48.8 24.7 all-gather.3
  75.4 38.4 all-gather.5
  115.7 42.3 all-gather.7
  177.8 40.6 reduce-scatter.3
  220.8 36.2 reduce-scatter.5
  259.6 26.9 reduce-scatter.7

commit v3 on v2

--- a/solution.py
+++ b/solution.py
@@ -6,8 +6,8 @@
 ADAPTER_SCALE = 2.0
 NORM_EPS = 1e-06
 LANES = 128
-OUT_TILES = (3, 5, 6)
-BACK_TILES = (6, 5, 3)
+OUT_TILES = (6, 8)
+BACK_TILES = (8, 6)
 
 
 def silu_parts(gate_val):

time: 386 us -> 361 us (0.935)
  matrix products: 53.8 us -> 31.7 us
  starting transfers between devices: 59.9 us -> 39.1 us
  blocking collectives: 91.3 us -> 111 us
    all_to_all x0 -> x1, blocking collectives: none -> 37.8 us  [send_back(): lax.all_to_all(summed.reshape(experts, capacity, -1), 'exp', split_axis=0...]
    all_to_all x3 -> x1, waiting for transfers between devices: 43.9 us -> 20.4 us  [send_back(): lax.all_to_all(summed.reshape(experts, capacity, -1), 'exp', split_axis=0...]
    dot_general x39 -> x27, matrix products: 50.7 us -> 28.9 us  [contract_trailing(): lax.dot_general(left, right, (((1,), (1,)), ((), ())), preferred_element_...]
    all_to_all x3 -> x1, starting transfers between devices: 32.1 us -> 10.7 us  [send_back(): lax.all_to_all(summed.reshape(experts, capacity, -1), 'exp', split_axis=0...]
    all_to_all x2 -> x1, blocking collectives: 53.2 us -> 34.9 us  [per_device(): lax.all_to_all(outgoing, 'exp', split_axis=0, concat_axis=0, tiled=True)]
    reduce_scatter x3 -> x2, waiting for transfers between devices: 32.5 us -> 40.3 us  [per_device(): lax.psum_scatter(partial_value, 'seq', scatter_dimension=0, tiled=False)]
    all_to_all x1, waiting for transfers between devices: 5.11 us -> 10.5 us  [per_device(): lax.all_to_all(lora_left, 'exp', split_axis=0, concat_axis=0, tiled=True)]
    all_to_all x1, waiting for transfers between devices: 19.7 us -> 25 us  [per_device(): lax.all_to_all(outgoing, 'exp', split_axis=0, concat_axis=0, tiled=True)]
  transfers between devices with their start and end apart: 14 -> 10, of which waited for: 10 -> 8; matrix products, arithmetic and copies ran while one was open for 11% -> 7% of each run, Pallas kernels for 0% -> 0%
where the time goes in v3:
time: 361 us; the launch traced here: 360 us
  waiting for transfers between devices  143 us (40%)
  blocking collectives  111 us (31%)
  starting transfers between devices  39.1 us (11%)
  matrix products  31.7 us (9%)
  between operations  14.2 us (4%)
  other arithmetic  11.5 us (3%)
  local copies, waits for them, and re-layouts  9.82 us (3%)
    reduce_scatter x2, waiting for transfers between devices, per_device(): lax.psum_scatter(partial_value, 'seq', scatter_dimension=0, tiled=False)  40.3 us
    all_to_all x1, blocking collectives, send_back(): lax.all_to_all(summed.reshape(experts, capacity, -1), 'exp', split_axis=0...  37.8 us
    all_to_all x1, blocking collectives, per_device(): lax.all_to_all(outgoing, 'exp', split_axis=0, concat_axis=0, tiled=True)  34.9 us
    all_gather x2, waiting for transfers between devices, per_device(): rows = lax.all_gather(incoming.reshape(-1, piece), 'seq', axis=0)  31.4 us
    dot_general x27, matrix products, contract_trailing(): lax.dot_general(left, right, (((1,), (1,)), ((), ())), preferred_element_...  28.9 us
    all_to_all x1, blocking collectives, per_device(): lax.all_to_all(lora_right, 'exp', split_axis=0, concat_axis=0, tiled=True)  27.6 us
    all_to_all x1, waiting for transfers between devices, per_device(): lax.all_to_all(outgoing, 'exp', split_axis=0, concat_axis=0, tiled=True)  25 us
    all_to_all x1, waiting for transfers between devices, send_back(): lax.all_to_all(summed.reshape(experts, capacity, -1), 'exp', split_axis=0...  20.4 us
  transfers between devices with their start and end apart: 10, of which 8 were waited for; matrix products, arithmetic and copies ran while one was open for 7% of the time, Pallas kernels for 0%

profile of v3, /device:TPU:51, one launch (start us, length us, event | category | flops | bytes accessed | tf_op | source)
XLA Modules:
  0.0 360.1 jit_solution(3798082654825693722)
XLA Ops:
  7.2 0.7 convert_element_type.91
  8.0 0.8 maximum_maximum_fusion
  8.8 1.8 pad_maximum_fusion.2
  10.6 4.2 %all-to-all-start = ((bf16[4,8,7808]{2,1,0:T(8,128)(2,1)}), bf16[4,8,7808]{2,1,0:T(8,128)(2,1)S(1)}, u32[]{:S(2)}, u32[]{:S(2)}) async-start(bf16[4,8,7808]{2,1,0:T(8,128)(2,1)} %pad_maximum_fusion.2), calls=%async_computation | async-start | bytes 999424 | tf_op jit(solution)/shard_map/all_to_all | solution.py:85
  15.0 5.5 %all-to-all-done = bf16[4,8,7808]{2,1,0:T(8,128)(2,1)S(1)} async-done(((bf16[4,8,7808]{2,1,0:T(8,128)(2,1)}), bf16[4,8,7808]{2,1,0:T(8,128)(2,1)S(1)}, u32[]{:S(2)}, u32[]{:S(2)}) %all-to-all-start) | async-done | bytes 499744 | tf_op jit(solution)/shard_map/all_to_all | solution.py:85
  21.1 0.4 fusion.5
  21.5 34.9 %all_to_all.40 = bf16[64,8,768]{2,1,0:T(8,128)(2,1)} all-to-all(bf16[64,8,768]{2,1,0:T(8,128)(2,1)S(1)} %fusion.5), channel_id=1, replica_groups=mesh['exp'=64,'seq'=4] {'exp'}, dimensions={0} | all-to-all | bytes 1572864 | tf_op jit(solution)/shard_map/all_to_all | solution.py:129
  56.5 1.4 fusion
  57.9 7.0 %all-to-all-start.2 = ((bf16[64,8,1024]{2,1,0:T(8,128)(2,1)}), bf16[64,8,1024]{2,1,0:T(8,128)(2,1)S(1)}, u32[]{:S(2)}, u32[]{:S(2)}) async-start(bf16[64,8,1024]{2,1,0:T(8,128)(2,1)} %fusion), calls=%async_computation.2 | async-start | bytes 2097152 | tf_op jit(solution)/shard_map/all_to_all | solution.py:129
  65.1 0.5 reshape.98
  65.6 0.3 copy.46
  66.1 1.1 maximum_bitcast_fusion
  67.2 25.0 %all-to-all-done.2 = bf16[64,8,1024]{2,1,0:T(8,128)(2,1)S(1)} async-done(((bf16[64,8,1024]{2,1,0:T(8,128)(2,1)}), bf16[64,8,1024]{2,1,0:T(8,128)(2,1)S(1)}, u32[]{:S(2)}, u32[]{:S(2)}) %all-to-all-start.2) | async-done | bytes 1048608 | tf_op jit(solution)/shard_map/all_to_all | solution.py:129
  92.2 1.0 copy-done.1
  93.3 7.1 %all-to-all-start.3 = ((bf16[64,32,128]{2,1,0:T(8,128)(2,1)}), bf16[64,32,128]{2,1,0:T(8,128)(2,1)S(1)}, u32[]{:S(2)}, u32[]{:S(2)}) async-start(bf16[64,32,128]{2,1,0:T(8,128)(2,1)} %maximum_bitcast_fusion), calls=%async_computation.3 | async-start | bytes 1048576 | tf_op jit(solution)/shard_map/all_to_all | solution.py:135
  100.7 1.8 fusion.18
  102.5 1.6 convolution_add_fusion.2
  104.1 1.4 convolution_add_fusion.1
  105.6 1.4 convolution_add_fusion
  107.0 10.5 %all-to-all-done.3 = bf16[64,32,128]{2,1,0:T(8,128)(2,1)S(1)} async-done(((bf16[64,32,128]{2,1,0:T(8,128)(2,1)}), bf16[64,32,128]{2,1,0:T(8,128)(2,1)S(1)}, u32[]{:S(2)}, u32[]{:S(2)}) %all-to-all-start.3) | async-done | bytes 524320 | tf_op jit(solution)/shard_map/all_to_all | solution.py:135
  117.5 31.4 %all-gather.5.cloned.1.call-done = bf16[4,512,1024]{2,1,0:T(8,128)(2,1)} async-done(((bf16[1,512,1024]{2,1,0:T(8,128)(2,1)}), bf16[4,512,1024]{2,1,0:T(8,128)(2,1)}) %all-gather.5.cloned.1.call-update) | async-done | bytes 4194320 | tf_op jit(solution)/shard_map/all_gather | solution.py:133
  148.8 2.0 convolution_add_fusion.6
  150.8 1.8 convolution_add_fusion.5
  152.7 1.5 convolution_add_fusion.4
  154.2 1.8 fusion.27
  156.0 0.4 copy-done.3
  156.4 0.5 fusion.42
  156.9 0.5 fusion.39
  157.4 0.5 fusion.36
  157.8 0.5 fusion.33
  158.3 0.6 copy-done.2
  158.9 0.5 fusion.1
  159.4 0.5 fusion.2
  159.9 0.5 fusion.3
  160.4 0.5 fusion.4
  160.9 2.2 pad_maximum_fusion
  163.2 1.4 fusion.66
  164.6 1.4 fusion.6
  166.0 1.4 fusion.63
  167.4 1.4 fusion.7
  168.8 1.4 fusion.60
  170.2 1.4 fusion.8
  171.6 1.4 fusion.57
  173.0 1.4 fusion.9
  174.5 1.9 pad_maximum_fusion.1
  176.4 36.1 %reduce-scatter.3.cloned.1.call-done = bf16[1,512,1024]{2,1,0:T(8,128)(2,1)} async-done(((bf16[4,512,1024]{2,1,0:T(8,128)(2,1)}), bf16[1,512,1024]{2,1,0:T(8,128)(2,1)}) %reduce-scatter.3.cloned.1.call-update) | async-done | bytes 1048592 | tf_op jit(solution)/shard_map/reduce_scatter | solution.py:177
  212.5 1.2 copy-done.5
  213.7 37.8 %all_to_all.41 = bf16[64,8,1024]{2,1,0:T(8,128)(2,1)S(1)} all-to-all(bf16[64,8,1024]{2,1,0:T(8,128)(2,1)S(1)} %bitcast.171), channel_id=1, replica_groups=mesh['exp'=64,'seq'=4] {'exp'}, dimensions={0} | all-to-all | bytes 2097152 | tf_op jit(solution)/shard_map/all_to_all | solution.py:153
  251.5 4.1 %reduce-scatter.5.cloned.1.call-done = bf16[1,512,768]{2,1,0:T(8,128)(2,1)} async-done(((bf16[4,512,768]{2,1,0:T(8,128)(2,1)}), bf16[1,512,768]{2,1,0:T(8,128)(2,1)}) %reduce-scatter.5.cloned.1.call-update) | async-done | bytes 786448 | tf_op jit(solution)/shard_map/reduce_scatter | solution.py:177
  255.7 10.7 %all-to-all-start.5 = ((bf16[64,8,768]{2,1,0:T(8,128)(2,1)}), bf16[64,8,768]{2,1,0:T(8,128)(2,1)S(1)}, u32[]{:S(2)}, u32[]{:S(2)}) async-start(bf16[64,8,768]{2,1,0:T(8,128)(2,1)} %bitcast.172), calls=%async_computation.7 | async-start | bytes 1572864 | tf_op jit(solution)/shard_map/all_to_all | solution.py:153
  266.5 0.8 dynamic-slice_convert_fusion
  267.7 0.3 convolution_bitcast_fusion
  268.0 20.4 %all-to-all-done.5 = bf16[64,8,768]{2,1,0:T(8,128)(2,1)S(1)} async-done(((bf16[64,8,768]{2,1,0:T(8,128)(2,1)}), bf16[64,8,768]{2,1,0:T(8,128)(2,1)S(1)}, u32[]{:S(2)}, u32[]{:S(2)}) %all-to-all-start.5) | async-done | bytes 786464 | tf_op jit(solution)/shard_map/all_to_all | solution.py:153
  289.3 10.6 %psum.7 = f32[32,128]{1,0:T(8,128)S(1)} all-reduce(f32[32,128]{1,0:T(8,128)S(1)} %concatenate.25), channel_id=1, replica_groups=mesh['exp'=64,'seq'=4] {'seq'}, use_global_device_ids=true, to_apply=%region_7.8 | all-reduce | flops 4096 | bytes 32768 | tf_op jit(solution)/shard_map/psum | solution.py:202
  300.1 0.8 fusion.79
  300.9 2.2 reshape.102
  303.6 0.4 maximum_bitcast_fusion.1
  304.0 27.6 %all_to_all.42 = bf16[64,32,128]{2,1,0:T(8,128)(2,1)S(1)} all-to-all(bf16[64,32,128]{2,1,0:T(8,128)(2,1)S(1)} %maximum_bitcast_fusion.1), channel_id=1, replica_groups=mesh['exp'=64,'seq'=4] {'exp'}, dimensions={0} | all-to-all | bytes 1048576 | tf_op jit(solution)/shard_map/all_to_all | solution.py:223
  331.6 5.7 %all-to-all-start.6 = ((bf16[4,8,1792]{2,1,0:T(8,128)(2,1)}), bf16[4,8,1792]{2,1,0:T(8,128)(2,1)S(1)}, u32[]{:S(2)}, u32[]{:S(2)}) async-start(bf16[4,8,1792]{2,1,0:T(8,128)(2,1)} %bitcast.56), calls=%async_computation.8 | async-start | bytes 229376 | tf_op jit(solution)/shard_map/all_to_all | solution.py:235
  337.8 4.1 %collective-permute-start = (f32[92,32]{0,1:T(8,128)S(1)}, f32[92,32]{0,1:T(8,128)S(1)}, u32[]{:S(2)}, u32[]{:S(2)}) collective-permute-start(f32[92,32]{0,1:T(8,128)S(1)} %pad_maximum_fusion.3), channel_id=1, source_target_pairs={{0,0},{1,64},{2,128},{3,192},{4,1},{5,65},{6,129},{7,193},{8,2},{9... | collective-permute-start | bytes 35336 | tf_op jit(solution)/shard_map/ppermute | solution.py:234
  341.9 9.7 %collective-permute-done = f32[92,32]{0,1:T(8,128)S(1)} collective-permute-done((f32[92,32]{0,1:T(8,128)S(1)}, f32[92,32]{0,1:T(8,128)S(1)}, u32[]{:S(2)}, u32[]{:S(2)}) %collective-permute-start) | collective-permute-done | bytes 11808 | tf_op jit(solution)/shard_map/ppermute | solution.py:234
  351.7 0.7 copy.51
  352.3 0.6 copy.54
  353.0 0.6 copy.55
  (66 shorter events, 4.0 us)
Async XLA Ops:
  7.2 260.2 %copy-start = (bf16[32,7168]{1,0:T(8,128)(2,1)S(1)}, bf16[32,7168]{1,0:T(8,128)(2,1)}, u32[]{:S(2)}) copy-start(bf16[32,7168]{1,0:T(8,128)(2,1)} %param.25) | copy-start | bytes 1376260
  10.6 9.9 %all-to-all-start = ((bf16[4,8,7808]{2,1,0:T(8,128)(2,1)}), bf16[4,8,7808]{2,1,0:T(8,128)(2,1)S(1)}, u32[]{:S(2)}, u32[]{:S(2)}) async-start(bf16[4,8,7808]{2,1,0:T(8,128)(2,1)} %pad_maximum_fusion.2), calls=%async_computation | async-start | bytes 999424 | tf_op jit(solution)/shard_map/all_to_all | solution.py:85
  14.9 85.8 %all-gather.3.cloned.1.call-start = ((), (), s32[]{:S(2)}) async-start(), calls=%async_computation.10 | async-start | bytes 3932160 | tf_op jit(solution)/shard_map/all_gather | solution.py:133
  57.9 34.3 %all-to-all-start.2 = ((bf16[64,8,1024]{2,1,0:T(8,128)(2,1)}), bf16[64,8,1024]{2,1,0:T(8,128)(2,1)S(1)}, u32[]{:S(2)}, u32[]{:S(2)}) async-start(bf16[64,8,1024]{2,1,0:T(8,128)(2,1)} %fusion), calls=%async_computation.2 | async-start | bytes 2097152 | tf_op jit(solution)/shard_map/all_to_all | solution.py:129
  64.9 83.9 %all-gather.5.cloned.1.call-start = ((), (), s32[]{:S(2)}) async-start(), calls=%async_computation.11 | async-start | bytes 5242880 | tf_op jit(solution)/shard_map/all_gather | solution.py:133
  92.2 1.0 copy-start.1
  93.3 24.2 %all-to-all-start.3 = ((bf16[64,32,128]{2,1,0:T(8,128)(2,1)}), bf16[64,32,128]{2,1,0:T(8,128)(2,1)S(1)}, u32[]{:S(2)}, u32[]{:S(2)}) async-start(bf16[64,32,128]{2,1,0:T(8,128)(2,1)} %maximum_bitcast_fusion), calls=%async_computation.3 | async-start | bytes 1048576 | tf_op jit(solution)/shard_map/all_to_all | solution.py:135
  100.4 112.1 %reduce-scatter.3.cloned.1.call-start = ((), (), s32[]{:S(2)}) async-start(), calls=%async_computation.12 | async-start | bytes 5242880 | tf_op jit(solution)/shard_map/reduce_scatter | solution.py:177
  100.7 3.5 copy-start.4
  107.0 47.2 %copy-start.9 = (bf16[1,512,256]{2,1,0:T(8,128)(2,1)S(1)}, bf16[1,512,256]{2,1,0:T(8,128)(2,1)}, u32[]{:S(2)}) copy-start(bf16[1,512,256]{2,1,0:T(8,128)(2,1)} %param.21) | copy-start | bytes 786436
  107.0 47.2 %copy-start.10 = (bf16[1,512,256]{2,1,0:T(8,128)(2,1)S(1)}, bf16[1,512,256]{2,1,0:T(8,128)(2,1)}, u32[]{:S(2)}) copy-start(bf16[1,512,256]{2,1,0:T(8,128)(2,1)} %param.22) | copy-start | bytes 786436
  117.5 36.7 %copy-start.6 = (bf16[64,32,128]{2,1,0:T(8,128)(2,1)}, bf16[64,32,128]{2,1,0:T(8,128)(2,1)S(1)}, u32[]{:S(2)}) copy-start(bf16[64,32,128]{2,1,0:T(8,128)(2,1)S(1)} %all-to-all-done.3) | copy-start | bytes 1572868
  148.8 3.8 %copy-start.8 = (bf16[4,512,1024]{2,1,0:T(8,128)(2,1)S(1)}, bf16[4,512,1024]{2,1,0:T(8,128)(2,1)}, u32[]{:S(2)}) copy-start(bf16[4,512,1024]{2,1,0:T(8,128)(2,1)} %all-gather.5.cloned.1.call-done) | copy-start | bytes 12582916
  154.2 2.2 copy-start.3
  156.9 2.0 copy-start.2
  163.1 92.5 %reduce-scatter.5.cloned.1.call-start = ((), (), s32[]{:S(2)}) async-start(), calls=%async_computation.13 | async-start | bytes 3932160 | tf_op jit(solution)/shard_map/reduce_scatter | solution.py:177
  212.5 1.2 copy-start.5
  255.7 32.7 %all-to-all-start.5 = ((bf16[64,8,768]{2,1,0:T(8,128)(2,1)}), bf16[64,8,768]{2,1,0:T(8,128)(2,1)S(1)}, u32[]{:S(2)}, u32[]{:S(2)}) async-start(bf16[64,8,768]{2,1,0:T(8,128)(2,1)} %bitcast.172), calls=%async_computation.7 | async-start | bytes 1572864 | tf_op jit(solution)/shard_map/all_to_all | solution.py:153
  268.0 69.2 %copy-start.7 = (bf16[64,32,128]{2,1,0:T(8,128)(2,1)S(1)}, bf16[64,32,128]{2,1,0:T(8,128)(2,1)}, u32[]{:S(2)}) copy-start(bf16[64,32,128]{2,1,0:T(8,128)(2,1)} %copy-done.6) | copy-start | bytes 1572868
  331.6 10.3 %all-to-all-start.6 = ((bf16[4,8,1792]{2,1,0:T(8,128)(2,1)}), bf16[4,8,1792]{2,1,0:T(8,128)(2,1)S(1)}, u32[]{:S(2)}, u32[]{:S(2)}) async-start(bf16[4,8,1792]{2,1,0:T(8,128)(2,1)} %bitcast.56), calls=%async_computation.8 | async-start | bytes 229376 | tf_op jit(solution)/shard_map/all_to_all | solution.py:235
  337.8 13.8 %collective-permute-start = (f32[92,32]{0,1:T(8,128)S(1)}, f32[92,32]{0,1:T(8,128)S(1)}, u32[]{:S(2)}, u32[]{:S(2)}) collective-permute-start(f32[92,32]{0,1:T(8,128)S(1)} %pad_maximum_fusion.3), channel_id=1, source_target_pairs={{0,0},{1,64},{2,128},{3,192},{4,1},{5,65},{6,129},{7,193},{8,2},{9... | collective-permute-start | bytes 35336 | tf_op jit(solution)/shard_map/ppermute | solution.py:234
Sparse Core Ops, SparseCore 0:
  56.6 39.1 all-gather.2
  97.6 51.1 all-gather.4
  163.3 49.1 reduce-scatter.2
  215.1 40.5 reduce-scatter.4

commit v4 on v3

--- a/solution.py
+++ b/solution.py
@@ -1,13 +1,17 @@
+import functools
+
 import jax
 import jax.numpy as jnp
 from jax import lax
+from jax.experimental import pallas as pl
+from jax.experimental.pallas import tpu as pltpu
 from jax.sharding import PartitionSpec as P
 
 ADAPTER_SCALE = 2.0
 NORM_EPS = 1e-06
 LANES = 128
-OUT_TILES = (6, 8)
 BACK_TILES = (8, 6)
+MESH = pl.DeviceIdType.MESH
 
 
 def silu_parts(gate_val):
@@ -36,6 +40,137 @@
 def by_column(array, parts):
     rows, columns = array.shape
     return array.reshape(rows, parts, columns // parts).transpose(1, 0, 2)
+
+
+def dispatch_kernel(
+    n_exp, n_seq, outgoing, rows, own_sem, send_sem, recv_sem, side_send, right_sem, left_sem,
+    far_send, far_sem,
+):
+    me, seq = lax.axis_index("exp"), lax.axis_index("seq")
+    right, left = lax.rem(seq + 1, n_seq), lax.rem(seq + n_seq - 1, n_seq)
+
+    barrier = pltpu.get_barrier_semaphore()
+
+    def greet(offset, carry):
+        pl.semaphore_signal(
+            barrier, inc=1, device_id=(lax.rem(me + offset, n_exp), seq), device_id_type=MESH
+        )
+        return carry
+
+    lax.fori_loop(1, n_exp, greet, 0)
+    for other in (right, left):
+        pl.semaphore_signal(barrier, inc=1, device_id=(me, other), device_id_type=MESH)
+    pl.semaphore_wait(barrier, n_exp + 1)
+
+    own = pltpu.make_async_copy(outgoing.at[me], rows.at[seq, me], own_sem)
+    own.start()
+
+    def over_exp(offset):
+        other = lax.rem(me + offset, n_exp)
+        return pltpu.make_async_remote_copy(
+            src_ref=outgoing.at[other],
+            dst_ref=rows.at[seq, me],
+            send_sem=send_sem.at[offset],
+            recv_sem=recv_sem.at[offset],
+            device_id=(other, seq),
+            device_id_type=MESH,
+        )
+
+    def start_over_exp(offset, carry):
+        over_exp(offset).start()
+        return carry
+
+    lax.fori_loop(1, n_exp, start_over_exp, 0)
+    own.wait()
+
+    def beside(offset, towards, columns, send, recv):
+        block = rows.at[columns, lax.rem(me - offset + n_exp, n_exp)]
+        return pltpu.make_async_remote_copy(
+            src_ref=block,
+            dst_ref=block,
+            send_sem=send,
+            recv_sem=recv,
+            device_id=(me, towards),
+            device_id_type=MESH,
+        )
+
+    def to_right(offset):
+        return beside(offset, right, seq, side_send.at[0, offset], right_sem.at[offset])
+
+    def to_left(offset):
+        return beside(offset, left, seq, side_send.at[1, offset], left_sem.at[offset])
+
+    def onward_right(offset):
+        return beside(offset, right, left, far_send.at[offset], far_sem.at[offset])
+
+    def onward_left(offset):
+        return beside(offset, left, right, far_send.at[offset], far_sem.at[offset])
+
+    def spread(offset):
+        to_right(offset).start()
+        to_left(offset).start()
+
+    def onward(pair):
+        to_right(2 * pair).wait_recv()
+        onward_right(2 * pair).start()
+        to_left(2 * pair).wait_recv()
+        to_right(2 * pair + 1).wait_recv()
+        to_left(2 * pair + 1).wait_recv()
+        onward_left(2 * pair + 1).start()
+
+    def arrive(offset):
+        over_exp(offset).wait_recv()
+        spread(offset)
+
+    spread(0)
+    arrive(1)
+
+    def step(pair, carry):
+        arrive(2 * pair)
+        arrive(2 * pair + 1)
+        onward(pair - 1)
+        return carry
+
+    lax.fori_loop(1, n_exp // 2, step, 0)
+    onward(n_exp // 2 - 1)
+
+    def finish(pair, carry):
+        for offset in (2 * pair, 2 * pair + 1):
+            to_right(offset).wait_send()
+            to_left(offset).wait_send()
+        onward_right(2 * pair).wait()
+        onward_left(2 * pair + 1).wait()
+        return carry
+
+    lax.fori_loop(0, n_exp // 2, finish, 0)
+
+    def sent(offset, carry):
+        over_exp(offset).wait_send()
+        return carry
+
+    lax.fori_loop(1, n_exp, sent, 0)
+
+
+def dispatch(outgoing, n_exp, n_seq):
+    return pl.pallas_call(
+        functools.partial(dispatch_kernel, n_exp, n_seq),
+        out_shape=jax.ShapeDtypeStruct((n_seq,) + outgoing.shape, outgoing.dtype),
+        in_specs=[pl.BlockSpec(memory_space=pl.ANY)],
+        out_specs=pl.BlockSpec(memory_space=pl.ANY),
+        scratch_shapes=[
+            pltpu.SemaphoreType.DMA,
+            pltpu.SemaphoreType.DMA((n_exp,)),
+            pltpu.SemaphoreType.DMA((n_exp,)),
+            pltpu.SemaphoreType.DMA((2, n_exp)),
+            pltpu.SemaphoreType.DMA((n_exp,)),
+            pltpu.SemaphoreType.DMA((n_exp,)),
+            pltpu.SemaphoreType.DMA((n_exp,)),
+            pltpu.SemaphoreType.DMA((n_exp,)),
+        ],
+        compiler_params=pltpu.CompilerParams(
+            collective_id=0, has_side_effects=True, vmem_limit_bytes=1 << 20
+        ),
+    )(outgoing)
 
 
 def per_device(
@@ -120,26 +255,13 @@
     ).transpose(1, 0, 2)
 
     down = expert_down_weight[0]
+    outgoing = contract_leading(pick, grad).astype(jnp.bfloat16)
+    rows = dispatch(outgoing.reshape(experts, capacity, quarter), n_exp, n_seq)
+    rows = rows.reshape(n_seq, -1, quarter)
     hidden_grad = None
-    start = 0
-    for index, tiles in enumerate(OUT_TILES):
-        piece = tiles * LANES
-        outgoing = contract_leading(pick, grad[:, start : start + piece]).astype(jnp.bfloat16)
-        outgoing = outgoing.reshape(experts, capacity, piece)
-        incoming = lax.all_to_all(outgoing, "exp", split_axis=0, concat_axis=0, tiled=True)
-        last = index == len(OUT_TILES) - 1
-        if last:
-            incoming, lora_left = lax.optimization_barrier((incoming, lora_left))
-        rows = lax.all_gather(incoming.reshape(-1, piece), "seq", axis=0)
-        if last:
-            lora_left = lax.all_to_all(lora_left, "exp", split_axis=0, concat_axis=0, tiled=True)
-            rows, lora_left = lax.optimization_barrier((rows, lora_left))
-        for source in range(n_seq):
-            first = source * quarter + start
-            term = contract_trailing(rows[source], down[:, first : first + piece])
-            hidden_grad = term if hidden_grad is None else hidden_grad + term
-        start += piece
-
+    for source in range(n_seq):
+        term = contract_trailing(rows[source], down[:, source * quarter : (source + 1) * quarter])
+        hidden_grad = term if hidden_grad is None else hidden_grad + term
     activation, silu_slope = silu_parts(stored_gate_state[0].astype(jnp.float32))
     gate_grad = (hidden_grad * stored_up_state[0].astype(jnp.float32) * silu_slope).astype(
         jnp.bfloat16
@@ -174,8 +296,15 @@
             partial_value, summed, returned = lax.optimization_barrier(
                 (partial_value, summed, returned)
             )
+        else:
+            partial_value, lora_left = lax.optimization_barrier((partial_value, lora_left))
         following = lax.psum_scatter(partial_value, "seq", scatter_dimension=0, tiled=False)
-        if summed is not None:
+        if summed is None:
+            lora_left = lax.all_to_all(lora_left, "exp", split_axis=0, concat_axis=0, tiled=True)
+            gate_grad, up_grad, lora_left = lax.optimization_barrier(
+                (gate_grad, up_grad, lora_left)
+            )
+        else:
             send_back(summed)
         start, summed = start + piece, following
     send_back(summed)

time: 361 us -> 342 us (0.947)
  waiting for transfers between devices: 143 us -> 48.2 us
  Pallas kernels: 0 us -> 90.8 us
  starting transfers between devices: 39.1 us -> 24.8 us
    pallas_call x0 -> x1, Pallas kernels: none -> 90.8 us  [dispatch(): pl.pallas_call(functools.partial(dispatch_kernel, n_exp, n_seq), out_shap...]
    all_to_all x2 -> x0, waiting for transfers between devices: 35.5 us -> none  [the longest x1 25 us: per_device(): lax.all_to_all(outgoing, 'exp', split_axis=0, concat_axis=0, tiled=True)]
    all_gather x2 -> x0, waiting for transfers between devices: 31.4 us -> none  [per_device(): rows = lax.all_gather(incoming.reshape(-1, piece), 'seq', axis=0)]
    reduce_scatter x2, waiting for transfers between devices: 40.3 us -> 12.7 us  [per_device(): lax.psum_scatter(partial_value, 'seq', scatter_dimension=0, tiled=False)]
    all_to_all x2 -> x0, starting transfers between devices: 14.1 us -> none  [the longest x1 7.14 us: per_device(): lax.all_to_all(lora_left, 'exp', split_axis=0, concat_axis=0, tiled=True)]
    dot_general x27 -> x23, matrix products: 28.9 us -> 27.3 us  [contract_trailing(): lax.dot_general(left, right, (((1,), (1,)), ((), ())), preferred_element_...]
  transfers between devices with their start and end apart: 10 -> 6, of which waited for: 8 -> 5; matrix products, arithmetic and copies ran while one was open for 7% -> 5% of each run, Pallas kernels for 0% -> 0%
where the time goes in v4:
time: 342 us; the launch traced here: 340 us
  blocking collectives  111 us (32%)
  Pallas kernels  90.8 us (27%)
  waiting for transfers between devices  48.2 us (14%)
  matrix products  29 us (8%)
  starting transfers between devices  24.8 us (7%)
  between operations  14.4 us (4%)
  local copies, waits for them, and re-layouts  11 us (3%)
  other arithmetic  10.8 us (3%)
    pallas_call x1, Pallas kernels, dispatch(): pl.pallas_call(functools.partial(dispatch_kernel, n_exp, n_seq), out_shap...  90.8 us
    all_to_all x1, blocking collectives, send_back(): lax.all_to_all(summed.reshape(experts, capacity, -1), 'exp', split_axis=0...  37.8 us
    all_to_all x1, blocking collectives, per_device(): lax.all_to_all(lora_left, 'exp', split_axis=0, concat_axis=0, tiled=True)  35.4 us
    all_to_all x1, blocking collectives, per_device(): lax.all_to_all(lora_right, 'exp', split_axis=0, concat_axis=0, tiled=True)  27.6 us
    dot_general x23, matrix products, contract_trailing(): lax.dot_general(left, right, (((1,), (1,)), ((), ())), preferred_element_...  27.3 us
    all_to_all x1, waiting for transfers between devices, send_back(): lax.all_to_all(summed.reshape(experts, capacity, -1), 'exp', split_axis=0...  20.3 us
    reduce_scatter x2, waiting for transfers between devices, per_device(): lax.psum_scatter(partial_value, 'seq', scatter_dimension=0, tiled=False)  12.7 us
    all_to_all x1, starting transfers between devices, send_back(): lax.all_to_all(summed.reshape(experts, capacity, -1), 'exp', split_axis=0...  10.7 us
  transfers between devices with their start and end apart: 6, of which 5 were waited for; matrix products, arithmetic and copies ran while one was open for 5% of the time, Pallas kernels for 0%

profile of v4, /device:TPU:51, one launch (start us, length us, event | category | flops | bytes accessed | tf_op | source)
XLA Modules:
  0.0 340.4 jit_solution(15782512254662145026)
XLA Ops:
  7.2 0.7 convert_element_type.88
  8.0 0.8 maximum_maximum_fusion
  8.8 1.9 pad_maximum_fusion.2
  10.6 4.2 %all-to-all-start = ((bf16[4,8,7808]{2,1,0:T(8,128)(2,1)}), bf16[4,8,7808]{2,1,0:T(8,128)(2,1)S(1)}, u32[]{:S(2)}, u32[]{:S(2)}) async-start(bf16[4,8,7808]{2,1,0:T(8,128)(2,1)} %pad_maximum_fusion.2), calls=%async_computation | async-start | bytes 999424 | tf_op jit(solution)/shard_map/all_to_all | solution.py:220
  15.1 5.5 %all-to-all-done = bf16[4,8,7808]{2,1,0:T(8,128)(2,1)S(1)} async-done(((bf16[4,8,7808]{2,1,0:T(8,128)(2,1)}), bf16[4,8,7808]{2,1,0:T(8,128)(2,1)S(1)}, u32[]{:S(2)}, u32[]{:S(2)}) %all-to-all-start) | async-done | bytes 499744 | tf_op jit(solution)/shard_map/all_to_all | solution.py:220
  20.6 0.2 select_reduce_fusion.1
  20.8 0.2 select_reduce_fusion
  21.1 0.7 fusion.outgoing
  21.8 90.8 %shard_map.148 = bf16[4,64,8,1792]{3,2,1,0:T(8,128)(2,1)S(1)} custom-call(bf16[64,8,1792]{2,1,0:T(8,128)(2,1)S(1)} %fusion.outgoing), custom_call_target="tpu_custom_call" | custom-call | tf_op jit(solution)/shard_map/pallas_call | solution.py:155
  112.6 0.7 fusion.1
  113.3 0.7 fusion.3
  114.0 0.7 fusion.5
  114.7 0.8 fusion.42
  115.6 1.2 copy-done.5
  116.8 1.8 fusion.44
  118.6 1.8 fusion.47
  120.4 1.8 fusion.50
  122.2 0.5 fusion.53
  122.7 1.4 reshape.103
  124.0 1.5 copy.46
  125.6 2.4 fusion.16
  127.9 1.5 fusion.15
  129.5 1.5 fusion.14
  131.0 1.5 fusion.13
  132.6 0.3 maximum_bitcast_fusion
  133.0 2.2 pad_maximum_fusion
  135.3 35.4 %all_to_all.30 = bf16[64,32,128]{2,1,0:T(8,128)(2,1)} all-to-all(bf16[64,32,128]{2,1,0:T(8,128)(2,1)S(1)} %maximum_bitcast_fusion), channel_id=1, replica_groups=mesh['exp'=64,'seq'=4] {'exp'}, dimensions={0} | all-to-all | bytes 1048576 | tf_op jit(solution)/shard_map/all_to_all | solution.py:303
  170.7 1.4 fusion.64
  172.1 1.4 fusion.20
  173.5 1.4 fusion.67
  174.9 1.4 fusion.19
  176.3 1.4 fusion.70
  177.7 1.4 fusion.18
  179.1 1.4 fusion.73
  180.5 1.4 fusion.17
  181.9 1.9 pad_maximum_fusion.1
  183.8 8.4 %reduce-scatter.3.cloned.1.call-done = bf16[1,512,1024]{2,1,0:T(8,128)(2,1)} async-done(((bf16[4,512,1024]{2,1,0:T(8,128)(2,1)}), bf16[1,512,1024]{2,1,0:T(8,128)(2,1)}) %reduce-scatter.3.cloned.1.call-update) | async-done | bytes 1048592 | tf_op jit(solution)/shard_map/reduce_scatter | solution.py:301
  192.3 1.2 copy-done.6
  193.5 37.8 %all_to_all.31 = bf16[64,8,1024]{2,1,0:T(8,128)(2,1)S(1)} all-to-all(bf16[64,8,1024]{2,1,0:T(8,128)(2,1)S(1)} %bitcast.157), channel_id=1, replica_groups=mesh['exp'=64,'seq'=4] {'exp'}, dimensions={0} | all-to-all | bytes 2097152 | tf_op jit(solution)/shard_map/all_to_all | solution.py:275
  231.3 4.3 %reduce-scatter.5.cloned.1.call-done = bf16[1,512,768]{2,1,0:T(8,128)(2,1)} async-done(((bf16[4,512,768]{2,1,0:T(8,128)(2,1)}), bf16[1,512,768]{2,1,0:T(8,128)(2,1)}) %reduce-scatter.5.cloned.1.call-update) | async-done | bytes 786448 | tf_op jit(solution)/shard_map/reduce_scatter | solution.py:301
  235.6 10.7 %all-to-all-start.3 = ((bf16[64,8,768]{2,1,0:T(8,128)(2,1)}), bf16[64,8,768]{2,1,0:T(8,128)(2,1)S(1)}, u32[]{:S(2)}, u32[]{:S(2)}) async-start(bf16[64,8,768]{2,1,0:T(8,128)(2,1)} %bitcast.158), calls=%async_computation.5 | async-start | bytes 1572864 | tf_op jit(solution)/shard_map/all_to_all | solution.py:275
  246.4 0.8 dynamic-slice_convert_fusion
  247.3 0.1 fusion.100
  247.4 0.2 fusion.103
  247.6 0.4 convolution_bitcast_fusion
  248.0 20.3 %all-to-all-done.3 = bf16[64,8,768]{2,1,0:T(8,128)(2,1)S(1)} async-done(((bf16[64,8,768]{2,1,0:T(8,128)(2,1)}), bf16[64,8,768]{2,1,0:T(8,128)(2,1)S(1)}, u32[]{:S(2)}, u32[]{:S(2)}) %all-to-all-start.3) | async-done | bytes 786464 | tf_op jit(solution)/shard_map/all_to_all | solution.py:275
  268.3 0.3 convolution_bitcast_fusion.1
  268.6 0.2 fusion.84
  268.8 0.1 fusion.96
  268.9 0.1 copy.47
  269.2 10.6 %psum.7 = f32[32,128]{1,0:T(8,128)S(1)} all-reduce(f32[32,128]{1,0:T(8,128)S(1)} %concatenate.25), channel_id=1, replica_groups=mesh['exp'=64,'seq'=4] {'seq'}, use_global_device_ids=true, to_apply=%region_7.8 | all-reduce | flops 4096 | bytes 32768 | tf_op jit(solution)/shard_map/psum | solution.py:331
  279.8 0.2 fusion.116
  280.0 0.8 fusion.86
  280.9 2.2 reshape.107
  283.1 0.3 copy.49
  283.5 0.4 maximum_bitcast_fusion.1
  283.9 27.6 %all_to_all.32 = bf16[64,32,128]{2,1,0:T(8,128)(2,1)S(1)} all-to-all(bf16[64,32,128]{2,1,0:T(8,128)(2,1)S(1)} %maximum_bitcast_fusion.1), channel_id=1, replica_groups=mesh['exp'=64,'seq'=4] {'exp'}, dimensions={0} | all-to-all | bytes 1048576 | tf_op jit(solution)/shard_map/all_to_all | solution.py:352
  311.5 5.7 %all-to-all-start.4 = ((bf16[4,8,1792]{2,1,0:T(8,128)(2,1)}), bf16[4,8,1792]{2,1,0:T(8,128)(2,1)S(1)}, u32[]{:S(2)}, u32[]{:S(2)}) async-start(bf16[4,8,1792]{2,1,0:T(8,128)(2,1)} %bitcast.49), calls=%async_computation.6 | async-start | bytes 229376 | tf_op jit(solution)/shard_map/all_to_all | solution.py:364
  317.2 0.3 convolution_bitcast_fusion.2
  317.7 4.1 %collective-permute-start = (f32[92,32]{0,1:T(8,128)S(1)}, f32[92,32]{0,1:T(8,128)S(1)}, u32[]{:S(2)}, u32[]{:S(2)}) collective-permute-start(f32[92,32]{0,1:T(8,128)S(1)} %pad_maximum_fusion.3), channel_id=1, source_target_pairs={{0,0},{1,64},{2,128},{3,192},{4,1},{5,65},{6,129},{7,193},{8,2},{9... | collective-permute-start | bytes 35336 | tf_op jit(solution)/shard_map/ppermute | solution.py:363
  321.8 9.7 %collective-permute-done = f32[92,32]{0,1:T(8,128)S(1)} collective-permute-done((f32[92,32]{0,1:T(8,128)S(1)}, f32[92,32]{0,1:T(8,128)S(1)}, u32[]{:S(2)}, u32[]{:S(2)}) %collective-permute-start) | collective-permute-done | bytes 11808 | tf_op jit(solution)/shard_map/ppermute | solution.py:363
  331.6 0.7 copy.51
  332.3 0.6 copy.54
  332.9 0.6 copy.55
  (52 shorter events, 1.5 us)
Async XLA Ops:
  7.2 240.1 %copy-start = (bf16[32,7168]{1,0:T(8,128)(2,1)S(1)}, bf16[32,7168]{1,0:T(8,128)(2,1)}, u32[]{:S(2)}) copy-start(bf16[32,7168]{1,0:T(8,128)(2,1)} %param.25) | copy-start | bytes 1376260
  10.6 9.9 %all-to-all-start = ((bf16[4,8,7808]{2,1,0:T(8,128)(2,1)}), bf16[4,8,7808]{2,1,0:T(8,128)(2,1)S(1)}, u32[]{:S(2)}, u32[]{:S(2)}) async-start(bf16[4,8,7808]{2,1,0:T(8,128)(2,1)} %pad_maximum_fusion.2), calls=%async_computation | async-start | bytes 999424 | tf_op jit(solution)/shard_map/all_to_all | solution.py:220
  14.9 177.4 %reduce-scatter.3.cloned.1.call-start = ((), (), s32[]{:S(2)}) async-start(), calls=%async_computation.8 | async-start | bytes 5242880 | tf_op jit(solution)/shard_map/reduce_scatter | solution.py:301
  20.5 92.1 %copy-start.3 = (bf16[4,8,7808]{2,1,0:T(8,128)(2,1)}, bf16[4,8,7808]{2,1,0:T(8,128)(2,1)S(1)}, u32[]{:S(2)}) copy-start(bf16[4,8,7808]{2,1,0:T(8,128)(2,1)S(1)} %all-to-all-done) | copy-start | bytes 1499140
  21.8 90.8 %copy-start.8 = (bf16[1,256,7168]{2,1,0:T(8,128)(2,1)S(1)}, bf16[1,256,7168]{2,1,0:T(8,128)(2,1)}, u32[]{:S(2)}) copy-start(bf16[1,256,7168]{2,1,0:T(8,128)(2,1)} %param.20) | copy-start | bytes 11010052
  113.3 1.4 copy-start.9
  113.3 1.4 copy-start.10
  114.7 2.0 copy-start.5
  124.0 3.9 %copy-start.2 = (f32[512,1024]{1,0:T(8,128)S(1)}, f32[512,1024]{1,0:T(8,128)}, u32[]{:S(2)}) copy-start(f32[512,1024]{1,0:T(8,128)} %fusion.47) | copy-start | bytes 6291460
  125.5 3.9 %copy-start.1 = (f32[512,1024]{1,0:T(8,128)S(1)}, f32[512,1024]{1,0:T(8,128)}, u32[]{:S(2)}) copy-start(f32[512,1024]{1,0:T(8,128)} %fusion.50) | copy-start | bytes 6291460
  135.2 100.4 %reduce-scatter.5.cloned.1.call-start = ((), (), s32[]{:S(2)}) async-start(), calls=%async_computation.9 | async-start | bytes 3932160 | tf_op jit(solution)/shard_map/reduce_scatter | solution.py:301
  183.8 63.5 %copy-start.4 = (bf16[4,8,7808]{2,1,0:T(8,128)(2,1)S(1)}, bf16[4,8,7808]{2,1,0:T(8,128)(2,1)}, u32[]{:S(2)}) copy-start(bf16[4,8,7808]{2,1,0:T(8,128)(2,1)} %copy-done.3) | copy-start | bytes 1499140
  192.3 1.2 copy-start.6
  235.6 32.7 %all-to-all-start.3 = ((bf16[64,8,768]{2,1,0:T(8,128)(2,1)}), bf16[64,8,768]{2,1,0:T(8,128)(2,1)S(1)}, u32[]{:S(2)}, u32[]{:S(2)}) async-start(bf16[64,8,768]{2,1,0:T(8,128)(2,1)} %bitcast.158), calls=%async_computation.5 | async-start | bytes 1572864 | tf_op jit(solution)/shard_map/all_to_all | solution.py:275
  248.0 69.2 %copy-start.7 = (bf16[64,32,128]{2,1,0:T(8,128)(2,1)S(1)}, bf16[64,32,128]{2,1,0:T(8,128)(2,1)}, u32[]{:S(2)}) copy-start(bf16[64,32,128]{2,1,0:T(8,128)(2,1)} %all_to_all.30) | copy-start | bytes 1572868
  311.5 10.4 %all-to-all-start.4 = ((bf16[4,8,1792]{2,1,0:T(8,128)(2,1)}), bf16[4,8,1792]{2,1,0:T(8,128)(2,1)S(1)}, u32[]{:S(2)}, u32[]{:S(2)}) async-start(bf16[4,8,1792]{2,1,0:T(8,128)(2,1)} %bitcast.49), calls=%async_computation.6 | async-start | bytes 229376 | tf_op jit(solution)/shard_map/all_to_all | solution.py:364
  317.7 13.8 %collective-permute-start = (f32[92,32]{0,1:T(8,128)S(1)}, f32[92,32]{0,1:T(8,128)S(1)}, u32[]{:S(2)}, u32[]{:S(2)}) collective-permute-start(f32[92,32]{0,1:T(8,128)S(1)} %pad_maximum_fusion.3), channel_id=1, source_target_pairs={{0,0},{1,64},{2,128},{3,192},{4,1},{5,65},{6,129},{7,193},{8,2},{9... | collective-permute-start | bytes 35336 | tf_op jit(solution)/shard_map/ppermute | solution.py:363
Sparse Core Ops, SparseCore 0:
  135.3 56.8 reduce-scatter.2
  195.0 40.5 reduce-scatter.4

commit v5 on v4

--- a/solution.py
+++ b/solution.py
@@ -10,7 +10,7 @@
 ADAPTER_SCALE = 2.0
 NORM_EPS = 1e-06
 LANES = 128
-BACK_TILES = (8, 6)
+BACK_TILES = (9, 5)
 MESH = pl.DeviceIdType.MESH
 
 
@@ -171,6 +171,63 @@
             collective_id=0, has_side_effects=True, vmem_limit_bytes=1 << 20
         ),
     )(outgoing)
+
+
+def exchange_kernel(n_exp, blocks, landed, own_sem, send_sem, recv_sem):
+    me, seq = lax.axis_index("exp"), lax.axis_index("seq")
+    barrier = pltpu.get_barrier_semaphore()
+
+    def greet(offset, carry):
+        pl.semaphore_signal(
+            barrier, inc=1, device_id=(lax.rem(me + offset, n_exp), seq), device_id_type=MESH
+        )
+        return carry
+
+    lax.fori_loop(1, n_exp, greet, 0)
+    pl.semaphore_wait(barrier, n_exp - 1)
+    own = pltpu.make_async_copy(blocks.at[me], landed.at[me], own_sem)
+    own.start()
+
+    def over_exp(offset):
+        other = lax.rem(me + offset, n_exp)
+        return pltpu.make_async_remote_copy(
+            src_ref=blocks.at[other],
+            dst_ref=landed.at[me],
+            send_sem=send_sem.at[offset],
+            recv_sem=recv_sem.at[offset],
+            device_id=(other, seq),
+            device_id_type=MESH,
+        )
+
+    def start(offset, carry):
+        over_exp(offset).start()
+        return carry
+
+    def finish(offset, carry):
+        over_exp(offset).wait()
+        return carry
+
+    lax.fori_loop(1, n_exp, start, 0)
+    own.wait()
+    lax.fori_loop(1, n_exp, finish, 0)
+
+
+def exchange(blocks, n_exp, collective_id):
+    return pl.pallas_call(
+        functools.partial(exchange_kernel, n_exp),
+        out_shape=jax.ShapeDtypeStruct(blocks.shape, blocks.dtype),
+        in_specs=[pl.BlockSpec(memory_space=pl.ANY)],
+        out_specs=pl.BlockSpec(memory_space=pl.ANY),
+        scratch_shapes=[
+            pltpu.SemaphoreType.DMA,
+            pltpu.SemaphoreType.DMA((n_exp,)),
+            pltpu.SemaphoreType.DMA((n_exp,)),
+        ],
+        compiler_params=pltpu.CompilerParams(
+            collective_id=collective_id, has_side_effects=True, vmem_limit_bytes=1 << 20
+        ),
+        cost_estimate=pl.CostEstimate(flops=0, bytes_accessed=50_000_000, transcendentals=0),
+    )(blocks)
 
 
 def per_device(
@@ -272,13 +329,7 @@
 
     def send_back(summed):
         returned.append(
-            lax.all_to_all(
-                summed.reshape(experts, capacity, -1),
-                "exp",
-                split_axis=0,
-                concat_axis=0,
-                tiled=True,
-            )
+            exchange(summed.reshape(experts, capacity, -1), n_exp, 1 + len(returned))
         )
 
     start, summed = 0, None
@@ -349,7 +400,7 @@
         ],
         axis=2,
     ).transpose(1, 0, 2)
-    lora_right = lax.all_to_all(lora_right, "exp", split_axis=0, concat_axis=0, tiled=True)
+    lora_right = exchange(lora_right, n_exp, 1 + len(BACK_TILES))
     products = contract_leading(
         lora_left.reshape(-1, LANES), lora_right.reshape(-1, LANES)
     )

time: 342 us -> 330 us (0.965)
  Pallas kernels: 90.8 us -> 174 us
  blocking collectives: 111 us -> 47.6 us
  waiting for transfers between devices: 48.2 us -> 28.2 us
  starting transfers between devices: 24.8 us -> 15.2 us
  matrix products: 29 us -> 22.4 us
  local copies, waits for them, and re-layouts: 11 us -> 14.7 us
    pallas_call x0 -> x3, Pallas kernels: none -> 85 us  [exchange(): pl.pallas_call(functools.partial(exchange_kernel, n_exp), out_shape=jax.S...]
    all_to_all x2 -> x0, blocking collectives: 65.4 us -> none  [the longest x1 37.8 us: send_back(): lax.all_to_all(summed.reshape(experts, capacity, -1), 'exp', split_axis=0...]
    all_to_all x1 -> x0, waiting for transfers between devices: 20.3 us -> none  [send_back(): lax.all_to_all(summed.reshape(experts, capacity, -1), 'exp', split_axis=0...]
    all_to_all x1 -> x0, starting transfers between devices: 10.7 us -> none  [send_back(): lax.all_to_all(summed.reshape(experts, capacity, -1), 'exp', split_axis=0...]
    dot_general x23, matrix products: 27.3 us -> 20.8 us  [contract_trailing(): lax.dot_general(left, right, (((1,), (1,)), ((), ())), preferred_element_...]
  transfers between devices with their start and end apart: 6 -> 5, of which waited for: 5 -> 4; matrix products, arithmetic and copies ran while one was open for 5% -> 5% of each run, Pallas kernels for 0% -> 11%
where the time goes in v5:
time: 330 us; the launch traced here: 328 us
  Pallas kernels  174 us (53%)
  blocking collectives  47.6 us (14%)
  waiting for transfers between devices  28.2 us (9%)
  matrix products  22.4 us (7%)
  starting transfers between devices  15.2 us (5%)
  local copies, waits for them, and re-layouts  14.7 us (4%)
  between operations  14.4 us (4%)
  other arithmetic  11.9 us (4%)
    pallas_call x1, Pallas kernels, dispatch(): pl.pallas_call(functools.partial(dispatch_kernel, n_exp, n_seq), out_shap...  89.1 us
    pallas_call x3, Pallas kernels, exchange(): pl.pallas_call(functools.partial(exchange_kernel, n_exp), out_shape=jax.S...  85 us
    all_to_all x1, blocking collectives, per_device(): lax.all_to_all(lora_left, 'exp', split_axis=0, concat_axis=0, tiled=True)  37 us
    dot_general x23, matrix products, contract_trailing(): lax.dot_general(left, right, (((1,), (1,)), ((), ())), preferred_element_...  20.8 us
    reduce_scatter x2, waiting for transfers between devices, per_device(): lax.psum_scatter(partial_value, 'seq', scatter_dimension=0, tiled=False)  14.1 us
    psum x1, blocking collectives, per_device(): sums = lax.psum(sums, 'seq')  10.6 us
    ppermute x1, waiting for transfers between devices, per_device(): total = lax.ppermute(total, ('exp', 'seq'), route)  8.53 us
  transfers between devices with their start and end apart: 5, of which 4 were waited for; matrix products, arithmetic and copies ran while one was open for 5% of the time, Pallas kernels for 11%

profile of v5, /device:TPU:51, one launch (start us, length us, event | category | flops | bytes accessed | tf_op | source)
XLA Modules:
  0.0 328.4 jit_solution(7910139054675014892)
XLA Ops:
  7.2 0.7 convert_element_type.88
  8.0 0.8 maximum_maximum_fusion
  8.8 1.9 pad_maximum_fusion.2
  10.6 4.2 %all-to-all-start = ((bf16[4,8,7808]{2,1,0:T(8,128)(2,1)}), bf16[4,8,7808]{2,1,0:T(8,128)(2,1)S(1)}, u32[]{:S(2)}, u32[]{:S(2)}) async-start(bf16[4,8,7808]{2,1,0:T(8,128)(2,1)} %pad_maximum_fusion.2), calls=%async_computation | async-start | bytes 999424 | tf_op jit(solution)/shard_map/all_to_all | solution.py:277
  15.1 5.5 %all-to-all-done = bf16[4,8,7808]{2,1,0:T(8,128)(2,1)S(1)} async-done(((bf16[4,8,7808]{2,1,0:T(8,128)(2,1)}), bf16[4,8,7808]{2,1,0:T(8,128)(2,1)S(1)}, u32[]{:S(2)}, u32[]{:S(2)}) %all-to-all-start) | async-done | bytes 499744 | tf_op jit(solution)/shard_map/all_to_all | solution.py:277
  20.6 0.2 select_reduce_fusion.1
  20.8 0.2 select_reduce_fusion
  21.1 0.7 fusion.4.outgoing
  21.8 89.1 %shard_map.148 = bf16[4,64,8,1792]{3,2,1,0:T(8,128)(2,1)S(1)} custom-call(bf16[64,8,1792]{2,1,0:T(8,128)(2,1)S(1)} %fusion.4.outgoing), custom_call_target="tpu_custom_call" | custom-call | tf_op jit(solution)/shard_map/pallas_call | solution.py:155
  110.9 0.7 fusion.11
  111.6 0.7 fusion.13
  112.3 0.7 fusion.9
  113.0 0.2 copy-done.11
  113.3 0.8 fusion.70
  114.2 1.2 copy-done.8
  115.3 0.5 fusion.52
  115.9 0.5 fusion.49
  116.4 0.5 fusion.46
  117.0 0.5 fusion.43
  117.5 0.7 slice.172
  118.3 0.8 copy-done.7
  119.1 0.5 fusion.8
  119.7 0.6 fusion.7
  120.2 1.6 fusion.6
  121.8 1.6 fusion.5
  123.4 2.3 reshape.103
  125.7 1.5 copy.47
  127.3 1.1 maximum_bitcast_fusion
  128.5 2.5 pad_maximum_fusion
  131.0 1.0 copy-done.9
  132.0 37.0 %all_to_all.15 = bf16[64,32,128]{2,1,0:T(8,128)(2,1)S(1)} all-to-all(bf16[64,32,128]{2,1,0:T(8,128)(2,1)S(1)} %copy-done.9), channel_id=1, replica_groups=mesh['exp'=64,'seq'=4] {'exp'}, dimensions={0} | all-to-all | bytes 1048576 | tf_op jit(solution)/shard_map/all_to_all | solution.py:354
  168.9 1.4 fusion.81
  170.3 1.4 fusion.28
  171.7 1.4 fusion.78
  173.1 1.4 fusion.27
  174.5 1.4 fusion.75
  175.8 1.4 fusion.26
  177.2 1.4 fusion.72
  178.6 1.4 fusion.25
  180.0 1.9 pad_maximum_fusion.1
  181.9 12.0 %reduce-scatter.3.cloned.1.call-done = bf16[1,512,1152]{2,1,0:T(8,128)(2,1)} async-done(((bf16[4,512,1152]{2,1,0:T(8,128)(2,1)}), bf16[1,512,1152]{2,1,0:T(8,128)(2,1)}) %reduce-scatter.3.cloned.1.call-update) | async-done | bytes 1179664 | tf_op jit(solution)/shard_map/reduce_scatter | solution.py:352
  194.1 0.8 dynamic-slice_convert_fusion
  195.2 0.2 fusion.111
  195.4 35.0 %shard_map.149 = bf16[64,8,1152]{2,1,0:T(8,128)(2,1)S(1)} custom-call(bf16[64,8,1152]{2,1,0:T(8,128)(2,1)S(1)} %bitcast.149), custom_call_target="tpu_custom_call" | custom-call | bytes 50000000 | tf_op jit(solution)/shard_map/pallas_call | solution.py:216
  230.4 0.3 convolution_bitcast_fusion
  230.8 2.1 reduce-scatter.5.cloned.1.call-done
  232.9 1.1 copy-done.2
  233.9 24.1 %shard_map.150 = bf16[64,8,640]{2,1,0:T(8,128)(2,1)S(1)} custom-call(bf16[64,8,640]{2,1,0:T(8,128)(2,1)S(1)} %bitcast.150), custom_call_target="tpu_custom_call" | custom-call | bytes 50000000 | tf_op jit(solution)/shard_map/pallas_call | solution.py:216
  258.1 0.3 convolution_bitcast_fusion.1
  258.3 0.2 fusion.92
  258.9 10.6 %psum.7 = f32[32,128]{1,0:T(8,128)S(1)} all-reduce(f32[32,128]{1,0:T(8,128)S(1)} %concatenate.25), channel_id=1, replica_groups=mesh['exp'=64,'seq'=4] {'seq'}, use_global_device_ids=true, to_apply=%region_7.8 | all-reduce | flops 4096 | bytes 32768 | tf_op jit(solution)/shard_map/psum | solution.py:382
  269.5 0.2 fusion.124
  269.7 0.8 fusion.94
  270.6 2.2 reshape.107
  272.8 0.3 copy.50
  273.3 0.4 maximum_bitcast_fusion.1.blocks
  273.6 25.9 %shard_map.151 = bf16[64,32,128]{2,1,0:T(8,128)(2,1)S(1)} custom-call(bf16[64,32,128]{2,1,0:T(8,128)(2,1)S(1)} %maximum_bitcast_fusion.1.blocks), custom_call_target="tpu_custom_call" | custom-call | bytes 50000000 | tf_op jit(solution)/shard_map/pallas_call | solution.py:216
  299.5 0.3 convolution_bitcast_fusion.2
  300.0 5.7 %all-to-all-start.2 = ((bf16[4,8,1792]{2,1,0:T(8,128)(2,1)}), bf16[4,8,1792]{2,1,0:T(8,128)(2,1)S(1)}, u32[]{:S(2)}, u32[]{:S(2)}) async-start(bf16[4,8,1792]{2,1,0:T(8,128)(2,1)} %bitcast.49), calls=%async_computation.4 | async-start | bytes 229376 | tf_op jit(solution)/shard_map/all_to_all | solution.py:415
  305.8 5.2 %collective-permute-start = (f32[92,32]{0,1:T(8,128)S(1)}, f32[92,32]{0,1:T(8,128)S(1)}, u32[]{:S(2)}, u32[]{:S(2)}) collective-permute-start(f32[92,32]{0,1:T(8,128)S(1)} %pad_maximum_fusion.3), channel_id=1, source_target_pairs={{0,0},{1,64},{2,128},{3,192},{4,1},{5,65},{6,129},{7,193},{8,2},{9... | collective-permute-start | bytes 35336 | tf_op jit(solution)/shard_map/ppermute | solution.py:414
  311.0 8.5 %collective-permute-done = f32[92,32]{0,1:T(8,128)S(1)} collective-permute-done((f32[92,32]{0,1:T(8,128)S(1)}, f32[92,32]{0,1:T(8,128)S(1)}, u32[]{:S(2)}, u32[]{:S(2)}) %collective-permute-start) | collective-permute-done | bytes 11808 | tf_op jit(solution)/shard_map/ppermute | solution.py:414
  319.6 0.7 copy.52
  320.3 0.6 copy.55
  320.9 0.6 copy.56
  (55 shorter events, 1.9 us)
Async XLA Ops:
  7.2 187.9 %copy-start = (bf16[32,7168]{1,0:T(8,128)(2,1)S(1)}, bf16[32,7168]{1,0:T(8,128)(2,1)}, u32[]{:S(2)}) copy-start(bf16[32,7168]{1,0:T(8,128)(2,1)} %param.25) | copy-start | bytes 1376260
  10.6 9.9 %all-to-all-start = ((bf16[4,8,7808]{2,1,0:T(8,128)(2,1)}), bf16[4,8,7808]{2,1,0:T(8,128)(2,1)S(1)}, u32[]{:S(2)}, u32[]{:S(2)}) async-start(bf16[4,8,7808]{2,1,0:T(8,128)(2,1)} %pad_maximum_fusion.2), calls=%async_computation | async-start | bytes 999424 | tf_op jit(solution)/shard_map/all_to_all | solution.py:277
  14.9 179.1 %reduce-scatter.3.cloned.1.call-start = ((), (), s32[]{:S(2)}) async-start(), calls=%async_computation.5 | async-start | bytes 5898240 | tf_op jit(solution)/shard_map/reduce_scatter | solution.py:352
  20.5 97.7 %copy-start.5 = (bf16[4,8,7808]{2,1,0:T(8,128)(2,1)}, bf16[4,8,7808]{2,1,0:T(8,128)(2,1)S(1)}, u32[]{:S(2)}) copy-start(bf16[4,8,7808]{2,1,0:T(8,128)(2,1)S(1)} %all-to-all-done) | copy-start | bytes 1499140
  21.8 89.1 %copy-start.10 = (bf16[1,256,7168]{2,1,0:T(8,128)(2,1)S(1)}, bf16[1,256,7168]{2,1,0:T(8,128)(2,1)}, u32[]{:S(2)}) copy-start(bf16[1,256,7168]{2,1,0:T(8,128)(2,1)} %param.20) | copy-start | bytes 11010052
  112.3 1.0 copy-start.11
  112.3 1.0 copy-start.12
  113.3 2.0 copy-start.8
  117.0 2.1 copy-start.7
  125.7 2.8 copy-start.3
  125.7 2.8 copy-start.4
  130.9 1.0 copy-start.9
  130.9 101.9 %reduce-scatter.5.cloned.1.call-start = ((), (), s32[]{:S(2)}) async-start(), calls=%async_computation.6 | async-start | bytes 3276800 | tf_op jit(solution)/shard_map/reduce_scatter | solution.py:352
  181.9 13.1 %copy-start.6 = (bf16[4,8,7808]{2,1,0:T(8,128)(2,1)S(1)}, bf16[4,8,7808]{2,1,0:T(8,128)(2,1)}, u32[]{:S(2)}) copy-start(bf16[4,8,7808]{2,1,0:T(8,128)(2,1)} %copy-done.5) | copy-start | bytes 1499140
  194.0 1.4 copy-start.1
  232.9 1.1 copy-start.2
  300.0 20.3 %all-to-all-start.2 = ((bf16[4,8,1792]{2,1,0:T(8,128)(2,1)}), bf16[4,8,1792]{2,1,0:T(8,128)(2,1)S(1)}, u32[]{:S(2)}, u32[]{:S(2)}) async-start(bf16[4,8,1792]{2,1,0:T(8,128)(2,1)} %bitcast.49), calls=%async_computation.4 | async-start | bytes 229376 | tf_op jit(solution)/shard_map/all_to_all | solution.py:415
  305.8 13.8 %collective-permute-start = (f32[92,32]{0,1:T(8,128)S(1)}, f32[92,32]{0,1:T(8,128)S(1)}, u32[]{:S(2)}, u32[]{:S(2)}) collective-permute-start(f32[92,32]{0,1:T(8,128)S(1)} %pad_maximum_fusion.3), channel_id=1, source_target_pairs={{0,0},{1,64},{2,128},{3,192},{4,1},{5,65},{6,129},{7,193},{8,2},{9... | collective-permute-start | bytes 35336 | tf_op jit(solution)/shard_map/ppermute | solution.py:414
Sparse Core Ops, SparseCore 0:
  131.1 62.8 reduce-scatter.2
  196.5 36.2 reduce-scatter.4
